TPU v7x, 32 devices: a whole 2x2x4 slice. The times are simulated.
32 devices in a mesh: ctx: 8 (over z, x), head: 4 (over y, core).
Axes of the slice: x: 2, y: 2, z: 4, core: 2. Of those that a mesh axis runs over, the one named last changes fastest.
Arguments:
- queries: bfloat16 [256, 128, 128], P('head'), may hold values from -48 to 48
- keys: bfloat16 [8, 65536, 128], P('head', 'ctx'), may hold values from -6 to 6
- values: bfloat16 [8, 65536, 128], P('head', 'ctx'), may hold values from -6 to 6
- key_block_scale: float32 [8, 1024], P('head', 'ctx'), may hold values from 0.5 to 2
- value_block_scale: float32 [8, 1024], P('head', 'ctx'), may hold values from 0.5 to 2
- selection: int32 [8, 128], P('head'), may hold values from 0 to 1023, as said below
Outputs:
- attended: bfloat16 [256, 128, 128], P('ctx', 'head')
Inputs may be any that keep to these rules, and one draw needn't show every extreme that they name: `selection`: each row lists 128 distinct block numbers in increasing order. Of the blocks i * 128 to (i + 1) * 128 - 1, a row lists between 1 and 40, and exactly 40 for some i in every row.
All inputs are finite; a program needn't handle non-finite values.
Results may differ from a plain program's by a relative error of at most 0.017.
Values may be sent and summed in bfloat16 or wider, within the bound.
No kernel may reach another device: no remote copies, remote signals or barrier semaphores. Data moves between devices by JAX's collectives and lax.ppermute only.
A program may use at most 192 MiB of HBM per device.

v0:
```python
import jax
import jax.numpy as jnp
from jax import lax
from jax.sharding import PartitionSpec as P

HEAD_SIZE = 128
BLK = 64
MOST = 40


def head_partials(query_rows, key_head, value_head, key_scales, value_scales, chosen, base_block):
    local_blocks = key_head.shape[0] // BLK
    per_turn = max(1, 512 // BLK)
    key_blocks = key_head.reshape(local_blocks, BLK, HEAD_SIZE)
    value_blocks = value_head.reshape(local_blocks, BLK, HEAD_SIZE)
    first = jnp.sum(chosen < base_block)
    count = jnp.sum((chosen >= base_block) & (chosen < base_block + local_blocks))
    padded = jnp.concatenate([chosen, jnp.zeros((MOST + per_turn,), jnp.int32)])
    factor = 1.0 / HEAD_SIZE**0.5
    rows = query_rows.shape[0]

    def advance(turn, carry):
        row_peak, row_total, summed = carry
        block_ids = lax.dynamic_slice_in_dim(padded, first + turn * per_turn, per_turn) - base_block
        valid = turn * per_turn + jnp.arange(per_turn) < count
        block_ids = jnp.clip(block_ids, 0, local_blocks - 1)
        key_rows = key_blocks[block_ids].reshape(per_turn * BLK, HEAD_SIZE)
        value_rows = value_blocks[block_ids].reshape(per_turn * BLK, HEAD_SIZE)
        key_factor = jnp.repeat(
            key_scales[block_ids] * factor, BLK, total_repeat_length=per_turn * BLK
        )
        value_factor = jnp.repeat(value_scales[block_ids], BLK, total_repeat_length=per_turn * BLK)
        live = jnp.repeat(valid, BLK, total_repeat_length=per_turn * BLK)
        scores = (
            lax.dot_general(
                query_rows, key_rows, (((1,), (1,)), ((), ())), preferred_element_type=jnp.float32
            )
            * key_factor
        )
        scores = jnp.where(live, scores, -1e30)
        new_peak = jnp.maximum(row_peak, jnp.max(scores, axis=1))
        prob = jnp.where(live, jnp.exp(scores - new_peak[:, None]), 0.0)
        fading = jnp.exp(row_peak - new_peak)
        row_total = row_total * fading + jnp.sum(prob, axis=1)
        weights = (prob * value_factor).astype(jnp.bfloat16)
        summed = summed * fading[:, None] + jnp.dot(
            weights, value_rows, preferred_element_type=jnp.float32
        )
        return (new_peak, row_total, summed)

    start_state = (
        jnp.full((rows,), -1e30, jnp.float32),
        jnp.zeros((rows,), jnp.float32),
        jnp.zeros((rows, HEAD_SIZE), jnp.float32),
    )
    turns = (count + per_turn - 1) // per_turn
    return lax.fori_loop(0, turns, advance, start_state)


def on_device(queries, keys, values, key_block_scale, value_block_scale, selection):
    grouped_queries = lax.all_to_all(queries, "head", split_axis=1, concat_axis=0, tiled=True)
    token_count = grouped_queries.shape[0]
    local_heads = keys.shape[0]
    group_size = grouped_queries.shape[1] // local_heads
    ctx_index = lax.axis_index("ctx")
    base_block = ctx_index * (keys.shape[1] // BLK)
    peaks = []
    totals = []
    sums = []
    for head_index in range(local_heads):
        query_rows = grouped_queries[
            :, head_index * group_size : (head_index + 1) * group_size, :
        ].reshape(token_count * group_size, HEAD_SIZE)
        row_peak, row_total, summed = head_partials(
            query_rows,
            keys[head_index],
            values[head_index],
            key_block_scale[head_index],
            value_block_scale[head_index],
            selection[head_index],
            base_block,
        )
        peaks.append(row_peak.reshape(token_count, group_size))
        totals.append(row_total.reshape(token_count, group_size))
        sums.append(summed.reshape(token_count, group_size, HEAD_SIZE))
    row_peak = jnp.concatenate(peaks, axis=1)
    row_total = jnp.concatenate(totals, axis=1)
    summed = jnp.concatenate(sums, axis=1)
    highest = lax.pmax(row_peak, "ctx")
    fading = jnp.exp(row_peak - highest)
    mine_sum, mine_total = (
        lax.psum_scatter(
            (summed * fading[..., None]).astype(jnp.bfloat16),
            "ctx",
            scatter_dimension=0,
            tiled=True,
        ).astype(jnp.float32),
        lax.psum_scatter(
            (row_total * fading).astype(jnp.bfloat16), "ctx", scatter_dimension=0, tiled=True
        ).astype(jnp.float32),
    )
    result = mine_sum / mine_total[..., None]
    return result.astype(jnp.bfloat16)


def solution(mesh):
    return jax.shard_map(
        on_device,
        mesh=mesh,
        in_specs=(
            P("head", None, None),
            P("head", "ctx", None),
            P("head", "ctx", None),
            P("head", "ctx"),
            P("head", "ctx"),
            P("head", None),
        ),
        out_specs=P("ctx", "head", None),
        check_vma=False,
    )
```

profile of v0, /device:TPU:4, one launch (start us, length us, event | category | flops | bytes accessed | tf_op | source)
XLA Modules:
  0.0 500.1 jit_solution(3682192395469297319)
XLA Ops:
  25.6 12.6 %all-to-all-done = bf16[64,128,128]{2,0,1:T(8,128)(2,1)S(1)} async-done(((bf16[64,128,128]{2,0,1:T(8,128)(2,1)}), bf16[64,128,128]{2,0,1:T(8,128)(2,1)S(1)}, u32[]{:S(2)}, u32[]{:S(2)}) %all-to-all-start) | async-done | bytes 2097184 | tf_op jit(solution)/shard_map/all_to_all | solution.py:61
  41.4 111.1 %while.42 = (s32[]{:T(128)}, f32[4096]{0:T(1024)S(1)}, f32[4096]{0:T(1024)S(1)}, f32[4096,128]{1,0:T(8,128)}, s32[]{:T(128)}, /*index=5*/s32[]{:T(128)}, s32[]{:...) while((s32[]{:T(128)}, f32[4096]{0:T(1024)S(1)}, ...), condition=%wide.region_5.8_spmd, body=%wide.region_2.7_spmd.sunk | while | flops 1104187392 | bytes 65035200 | solution.py:57
  44.7 9.9 %select_select_fusion.10 = (f32[512]{0:T(512)S(1)}, f32[512]{0:T(512)S(1)}) fusion(f32[]{:T(128)} %bitcast.290, f32[]{:T(128)} %bitcast.291, f32[]{:T(128)} %bitcast.292, f32[]{:T(128)} %bitcast.293, f32[]{:T(128)} %bitcast.294, f32[]{:T(128)} %bitcast.295, f32[]{:T(128)} %bitcast.296, f32[]{:T(128)} %bitcast.297, ...), kind=kLoop, calls=%fused_computation.20.clone.1 | loop fusion | flops 15872 | bytes 6224 | tf_op jit(solution)/shard_map/while/body/jit(_take)/select_n | solution.py:32
  70.1 8.3 %convolution_add_fusion.4 = f32[4096,128]{1,0:T(8,128)} fusion(bf16[512,128]{1,0:T(8,128)(2,1)S(1)} %bitcast.359, f32[512,4096]{1,0:T(8,128)} %copy-done, f32[512]{0:T(512)S(1)} %get-tuple-element.1015, f32[4096]{0:T(1024)S(1)} %max.28, f32[512]{0:T(512)S(1)} %get-tuple-element.1003, pred[512]{0:T(512)(128)(4,1)S(1)} %select_select_fusion.11, ...), kind=kOutput, calls=%fused_computation.13.clone.1 | convolution fusion | flops 550502400 | bytes 12751360 | tf_op jit(solution)/shard_map/while/body/dot_general | solution.py:46
  81.7 9.9 %select_select_fusion.10 = (f32[512]{0:T(512)S(1)}, f32[512]{0:T(512)S(1)}) fusion(f32[]{:T(128)} %bitcast.290, f32[]{:T(128)} %bitcast.291, f32[]{:T(128)} %bitcast.292, f32[]{:T(128)} %bitcast.293, f32[]{:T(128)} %bitcast.294, f32[]{:T(128)} %bitcast.295, f32[]{:T(128)} %bitcast.296, f32[]{:T(128)} %bitcast.297, ...), kind=kLoop, calls=%fused_computation.20.clone.1 | loop fusion | flops 15872 | bytes 6224 | tf_op jit(solution)/shard_map/while/body/jit(_take)/select_n | solution.py:32
  107.2 8.3 %convolution_add_fusion.4 = f32[4096,128]{1,0:T(8,128)} fusion(bf16[512,128]{1,0:T(8,128)(2,1)S(1)} %bitcast.359, f32[512,4096]{1,0:T(8,128)} %copy-done, f32[512]{0:T(512)S(1)} %get-tuple-element.1015, f32[4096]{0:T(1024)S(1)} %max.28, f32[512]{0:T(512)S(1)} %get-tuple-element.1003, pred[512]{0:T(512)(128)(4,1)S(1)} %select_select_fusion.11, ...), kind=kOutput, calls=%fused_computation.13.clone.1 | convolution fusion | flops 550502400 | bytes 12751360 | tf_op jit(solution)/shard_map/while/body/dot_general | solution.py:46
  118.8 9.9 %select_select_fusion.10 = (f32[512]{0:T(512)S(1)}, f32[512]{0:T(512)S(1)}) fusion(f32[]{:T(128)} %bitcast.290, f32[]{:T(128)} %bitcast.291, f32[]{:T(128)} %bitcast.292, f32[]{:T(128)} %bitcast.293, f32[]{:T(128)} %bitcast.294, f32[]{:T(128)} %bitcast.295, f32[]{:T(128)} %bitcast.296, f32[]{:T(128)} %bitcast.297, ...), kind=kLoop, calls=%fused_computation.20.clone.1 | loop fusion | flops 15872 | bytes 6224 | tf_op jit(solution)/shard_map/while/body/jit(_take)/select_n | solution.py:32
  144.2 8.3 %convolution_add_fusion.4 = f32[4096,128]{1,0:T(8,128)} fusion(bf16[512,128]{1,0:T(8,128)(2,1)S(1)} %bitcast.359, f32[512,4096]{1,0:T(8,128)} %copy-done, f32[512]{0:T(512)S(1)} %get-tuple-element.1015, f32[4096]{0:T(1024)S(1)} %max.28, f32[512]{0:T(512)S(1)} %get-tuple-element.1003, pred[512]{0:T(512)(128)(4,1)S(1)} %select_select_fusion.11, ...), kind=kOutput, calls=%fused_computation.13.clone.1 | convolution fusion | flops 550502400 | bytes 12751360 | tf_op jit(solution)/shard_map/while/body/dot_general | solution.py:46
  152.9 173.2 %while.43 = (s32[]{:T(128)}, f32[4096]{0:T(1024)S(1)}, f32[4096]{0:T(1024)S(1)}, f32[4096,128]{1,0:T(8,128)S(1)}, s32[]{:T(128)}, /*index=5*/s32[]{:T(128)}, s32...) while((s32[]{:T(128)}, f32[4096]{0:T(1024)S(1)}, ...), condition=%wide.region_11.14_spmd, body=%wide.region_8.13_spmd.sunk | while | flops 1104187392 | bytes 65035200 | solution.py:57
  156.4 10.1 %select_select_fusion.12 = (f32[512]{0:T(512)S(1)}, f32[512]{0:T(512)S(1)}) fusion(f32[]{:T(128)} %bitcast.321, f32[]{:T(128)} %bitcast.322, f32[]{:T(128)} %bitcast.323, f32[]{:T(128)} %bitcast.324, f32[]{:T(128)} %bitcast.325, f32[]{:T(128)} %bitcast.326, f32[]{:T(128)} %bitcast.327, f32[]{:T(128)} %bitcast.328, ...), kind=kLoop, calls=%fused_computation.48.clone.1 | loop fusion | flops 15872 | bytes 6224 | tf_op jit(solution)/shard_map/while/body/jit(_take)/select_n | solution.py:32
  167.8 5.0 %select_select_fusion.13 = pred[512]{0:T(512)(128)(4,1)S(1)} fusion(pred[]{:T(512)} %bitcast.337, pred[]{:T(512)} %bitcast.338, pred[]{:T(512)} %bitcast.339, pred[]{:T(512)} %bitcast.340, pred[]{:T(512)} %bitcast.341, pred[]{:T(512)} %bitcast.342, pred[]{:T(512)} %bitcast.343, pred[]{:T(512)} %bitcast.344, s32[4,128]{1,0:T(4,128)S(1)} %get-tuple-element.1117, ...), kind=kLoop, calls=%fused_computation.50.clone.1 | loop fusion | flops 11776 | bytes 2584 | tf_op jit(solution)/shard_map/while/body/jit(_take)/select_n | solution.py:33
  182.0 5.6 %convolution_add_fusion.5 = f32[4096,128]{1,0:T(8,128)S(1)} fusion(bf16[512,128]{1,0:T(8,128)(2,1)S(1)} %bitcast.360, f32[512,4096]{1,0:T(8,128)} %copy-done.1, f32[512]{0:T(512)S(1)} %get-tuple-element.1059, f32[4096]{0:T(1024)S(1)} %max.29, f32[512]{0:T(512)S(1)} %get-tuple-element.1047, pred[512]{0:T(512)(128)(4,1)S(1)} %select_select_fusion.13, ...), kind=kOutput, calls=%fused_computation.41.clone.1 | convolution fusion | flops 550502400 | bytes 12751360 | tf_op jit(solution)/shard_map/while/body/dot_general | solution.py:46
  191.0 10.1 %select_select_fusion.12 = (f32[512]{0:T(512)S(1)}, f32[512]{0:T(512)S(1)}) fusion(f32[]{:T(128)} %bitcast.321, f32[]{:T(128)} %bitcast.322, f32[]{:T(128)} %bitcast.323, f32[]{:T(128)} %bitcast.324, f32[]{:T(128)} %bitcast.325, f32[]{:T(128)} %bitcast.326, f32[]{:T(128)} %bitcast.327, f32[]{:T(128)} %bitcast.328, ...), kind=kLoop, calls=%fused_computation.48.clone.1 | loop fusion | flops 15872 | bytes 6224 | tf_op jit(solution)/shard_map/while/body/jit(_take)/select_n | solution.py:32
  202.4 5.0 %select_select_fusion.13 = pred[512]{0:T(512)(128)(4,1)S(1)} fusion(pred[]{:T(512)} %bitcast.337, pred[]{:T(512)} %bitcast.338, pred[]{:T(512)} %bitcast.339, pred[]{:T(512)} %bitcast.340, pred[]{:T(512)} %bitcast.341, pred[]{:T(512)} %bitcast.342, pred[]{:T(512)} %bitcast.343, pred[]{:T(512)} %bitcast.344, s32[4,128]{1,0:T(4,128)S(1)} %get-tuple-element.1117, ...), kind=kLoop, calls=%fused_computation.50.clone.1 | loop fusion | flops 11776 | bytes 2584 | tf_op jit(solution)/shard_map/while/body/jit(_take)/select_n | solution.py:33
  216.6 5.6 %convolution_add_fusion.5 = f32[4096,128]{1,0:T(8,128)S(1)} fusion(bf16[512,128]{1,0:T(8,128)(2,1)S(1)} %bitcast.360, f32[512,4096]{1,0:T(8,128)} %copy-done.1, f32[512]{0:T(512)S(1)} %get-tuple-element.1059, f32[4096]{0:T(1024)S(1)} %max.29, f32[512]{0:T(512)S(1)} %get-tuple-element.1047, pred[512]{0:T(512)(128)(4,1)S(1)} %select_select_fusion.13, ...), kind=kOutput, calls=%fused_computation.41.clone.1 | convolution fusion | flops 550502400 | bytes 12751360 | tf_op jit(solution)/shard_map/while/body/dot_general | solution.py:46
  225.7 10.1 %select_select_fusion.12 = (f32[512]{0:T(512)S(1)}, f32[512]{0:T(512)S(1)}) fusion(f32[]{:T(128)} %bitcast.321, f32[]{:T(128)} %bitcast.322, f32[]{:T(128)} %bitcast.323, f32[]{:T(128)} %bitcast.324, f32[]{:T(128)} %bitcast.325, f32[]{:T(128)} %bitcast.326, f32[]{:T(128)} %bitcast.327, f32[]{:T(128)} %bitcast.328, ...), kind=kLoop, calls=%fused_computation.48.clone.1 | loop fusion | flops 15872 | bytes 6224 | tf_op jit(solution)/shard_map/while/body/jit(_take)/select_n | solution.py:32
  251.2 5.6 %convolution_add_fusion.5 = f32[4096,128]{1,0:T(8,128)S(1)} fusion(bf16[512,128]{1,0:T(8,128)(2,1)S(1)} %bitcast.360, f32[512,4096]{1,0:T(8,128)} %copy-done.1, f32[512]{0:T(512)S(1)} %get-tuple-element.1059, f32[4096]{0:T(1024)S(1)} %max.29, f32[512]{0:T(512)S(1)} %get-tuple-element.1047, pred[512]{0:T(512)(128)(4,1)S(1)} %select_select_fusion.13, ...), kind=kOutput, calls=%fused_computation.41.clone.1 | convolution fusion | flops 550502400 | bytes 12751360 | tf_op jit(solution)/shard_map/while/body/dot_general | solution.py:46
  260.3 10.1 %select_select_fusion.12 = (f32[512]{0:T(512)S(1)}, f32[512]{0:T(512)S(1)}) fusion(f32[]{:T(128)} %bitcast.321, f32[]{:T(128)} %bitcast.322, f32[]{:T(128)} %bitcast.323, f32[]{:T(128)} %bitcast.324, f32[]{:T(128)} %bitcast.325, f32[]{:T(128)} %bitcast.326, f32[]{:T(128)} %bitcast.327, f32[]{:T(128)} %bitcast.328, ...), kind=kLoop, calls=%fused_computation.48.clone.1 | loop fusion | flops 15872 | bytes 6224 | tf_op jit(solution)/shard_map/while/body/jit(_take)/select_n | solution.py:32
  285.8 5.6 %convolution_add_fusion.5 = f32[4096,128]{1,0:T(8,128)S(1)} fusion(bf16[512,128]{1,0:T(8,128)(2,1)S(1)} %bitcast.360, f32[512,4096]{1,0:T(8,128)} %copy-done.1, f32[512]{0:T(512)S(1)} %get-tuple-element.1059, f32[4096]{0:T(1024)S(1)} %max.29, f32[512]{0:T(512)S(1)} %get-tuple-element.1047, pred[512]{0:T(512)(128)(4,1)S(1)} %select_select_fusion.13, ...), kind=kOutput, calls=%fused_computation.41.clone.1 | convolution fusion | flops 550502400 | bytes 12751360 | tf_op jit(solution)/shard_map/while/body/dot_general | solution.py:46
  294.9 10.1 %select_select_fusion.12 = (f32[512]{0:T(512)S(1)}, f32[512]{0:T(512)S(1)}) fusion(f32[]{:T(128)} %bitcast.321, f32[]{:T(128)} %bitcast.322, f32[]{:T(128)} %bitcast.323, f32[]{:T(128)} %bitcast.324, f32[]{:T(128)} %bitcast.325, f32[]{:T(128)} %bitcast.326, f32[]{:T(128)} %bitcast.327, f32[]{:T(128)} %bitcast.328, ...), kind=kLoop, calls=%fused_computation.48.clone.1 | loop fusion | flops 15872 | bytes 6224 | tf_op jit(solution)/shard_map/while/body/jit(_take)/select_n | solution.py:32
  320.4 5.6 %convolution_add_fusion.5 = f32[4096,128]{1,0:T(8,128)S(1)} fusion(bf16[512,128]{1,0:T(8,128)(2,1)S(1)} %bitcast.360, f32[512,4096]{1,0:T(8,128)} %copy-done.1, f32[512]{0:T(512)S(1)} %get-tuple-element.1059, f32[4096]{0:T(1024)S(1)} %max.29, f32[512]{0:T(512)S(1)} %get-tuple-element.1047, pred[512]{0:T(512)(128)(4,1)S(1)} %select_select_fusion.13, ...), kind=kOutput, calls=%fused_computation.41.clone.1 | convolution fusion | flops 550502400 | bytes 12751360 | tf_op jit(solution)/shard_map/while/body/dot_general | solution.py:46
  326.3 33.0 %pmax.7 = f32[256,32]{0,1:T(8,128)S(1)} all-reduce(f32[256,32]{0,1:T(8,128)S(1)} %pad_maximum_fusion), channel_id=1, replica_groups=mesh['ctx'=8,'head'=4] {'ctx'}, use_global_device_ids=true, to_apply=%region_12.15 | all-reduce | flops 8192 | bytes 65536 | tf_op jit(solution)/shard_map/pmax | solution.py:89
  365.0 55.3 %reduce-scatter.7.cloned.1.call-done = bf16[32,32]{1,0:T(8,128)(2,1)} async-done(((bf16[256,32]{1,0:T(8,128)(2,1)}), bf16[32,32]{1,0:T(8,128)(2,1)}) %reduce-scatter.7.cloned.1.call-update) | async-done | bytes 2064
  421.3 70.1 %reduce-scatter.5.cloned.1.call-done = bf16[32,32,128]{2,1,0:T(8,128)(2,1)} async-done(((bf16[256,32,128]{2,1,0:T(8,128)(2,1)}), bf16[32,32,128]{2,1,0:T(8,128)(2,1)}) %reduce-scatter.5.cloned.1.call-update) | async-done | bytes 262160 | tf_op jit(solution)/shard_map/reduce_scatter | solution.py:92
  (203 shorter events, 165.1 us)
Async XLA Ops:
  6.5 8.0 %copy-start.3 = (s32[2,128]{1,0:T(2,128)S(1)}, s32[2,128]{1,0:T(2,128)}, u32[]{:S(2)}) copy-start(s32[2,128]{1,0:T(2,128)} %param.31) | copy-start | bytes 3076
  10.8 27.3 %all-to-all-start = ((bf16[64,128,128]{2,0,1:T(8,128)(2,1)}), bf16[64,128,128]{2,0,1:T(8,128)(2,1)S(1)}, u32[]{:S(2)}, u32[]{:S(2)}) async-start(bf16[64,128,128]{2,0,1:T(8,128)(2,1)} %copy.32), calls=%async_computation | async-start | bytes 4194304 | tf_op jit(solution)/shard_map/all_to_all | solution.py:61
  14.4 406.0 %reduce-scatter.7.cloned.1.call-start = ((), (), s32[]{:S(2)}) async-start(), calls=%async_computation.4 | async-start | bytes 73728
  16.6 4.6 copy-start.4
  16.6 4.6 copy-start.5
  39.5 1.9 copy-start.2
  64.7 3.2 copy-start
  101.8 3.2 copy-start
  138.8 3.2 copy-start
  176.6 3.2 copy-start.1
  211.2 3.2 copy-start.1
  245.8 3.2 copy-start.1
  280.4 3.2 copy-start.1
  315.0 3.2 copy-start.1
  360.5 130.9 %reduce-scatter.5.cloned.1.call-start = ((), (), s32[]{:S(2)}) async-start(), calls=%async_computation.3 | async-start | bytes 2359296 | tf_op jit(solution)/shard_map/reduce_scatter | solution.py:92
Sparse Core Ops, SparseCore 0:
  360.6 59.7 reduce-scatter.6
  423.9 67.4 reduce-scatter.4
where the time goes:
time: 504 us; the launch traced here: 500 us
  other arithmetic  155 us (31%)
  waiting for transfers between devices  138 us (27%)
  local copies, waits for them, and re-layouts  84.7 us (17%)
  matrix products  65.3 us (13%)
  blocking collectives  33 us (7%)
  between operations  14.9 us (3%)
  loops' own time  5.71 us (1%)
    select_n x8, other arithmetic, advance(): jnp.repeat(value_scales[block_ids], BLK, total_repeat_length=per_turn * BLK)  80.1 us
    reduce_scatter x1, waiting for transfers between devices, on_device(): lax.psum_scatter((summed * fading[..., None]).astype(jnp.bfloat16), 'ctx'...  70.1 us
    unnamed x3, waiting for transfers between devices  55.4 us
    dot_general x8, matrix products, advance(): jnp.dot(weights, value_rows, preferred_element_type=jnp.float32)  53.1 us
    select_n x8, other arithmetic, advance(): live = jnp.repeat(valid, BLK, total_repeat_length=per_turn * BLK)  40.4 us
    pmax x1, blocking collectives, on_device(): highest = lax.pmax(row_peak, 'ctx')  33 us
    reduce_sum x8, other arithmetic, advance(): row_total = row_total * fading + jnp.sum(prob, axis=1)  21.1 us
    gather x8, local copies, waits for them, and re-layouts, advance(): value_rows = value_blocks[block_ids].reshape(per_turn * BLK, HEAD_SIZE)  17.3 us
  transfers between devices with their start and end apart: 3, of which 3 were waited for; matrix products, arithmetic and copies ran while one was open for 3% of the time, Pallas kernels for 0%

commit v1 on v0

v1 whole, which is shorter than its diff:
```python
import functools
import math

import jax
import jax.numpy as jnp
from jax import lax
from jax.experimental import pallas as pl
from jax.experimental.pallas import tpu as pltpu
from jax.sharding import PartitionSpec as P


MOST = 40
LANES = 128
PACK = 16
PARTS = 3
PER_TILE = 8
NEG = -1e30
SAFE = 2.0**64

SMEM = pl.BlockSpec(memory_space=pltpu.SMEM)
VMEM = pl.BlockSpec(memory_space=pltpu.VMEM)
HBM = pl.BlockSpec(memory_space=pltpu.HBM)


def locate(sel_ref, g, bound):
    length = sel_ref.shape[1]

    def halve(_, span):
        low, high = span
        mid = (low + high) // 2
        below = jnp.logical_and(low < high, sel_ref[g, jnp.minimum(mid, length - 1)] < bound)
        rest = jnp.logical_or(below, low >= high)
        return jnp.where(below, mid + 1, low), jnp.where(rest, high, mid)

    span = (jnp.int32(0), jnp.int32(length))
    return lax.fori_loop(0, length.bit_length(), halve, span)[0]


def collect_kernel(block, local, where_ref, sel_ref, ks_ref, vs_ref, k_hbm, v_hbm, tiles, table, scales, vbuf, ksem, vsem):
    heads, _, width = k_hbm.shape
    most = (tiles.shape[0]) // heads
    keys = PER_TILE * block
    factor = math.log2(math.e) / math.sqrt(width)
    base = where_ref[0]
    spans = []
    start = jnp.int32(0)
    for g in range(heads):
        first = locate(sel_ref, g, base)
        count = locate(sel_ref, g, base + local) - first
        turns = jnp.minimum((count + PER_TILE - 1) // PER_TILE, most)
        table[g] = start
        spans.append((first, count, turns, start))
        start = start + turns
    table[heads] = start

    for g in range(heads):
        first, count, turns, start = spans[g]

        def fetch(t, _, g=g, first=first, count=count, start=start):
            i = start + t
            for b in range(PER_TILE):
                slot = t * PER_TILE + b
                at = sel_ref[g, first + jnp.minimum(slot, count - 1)] - base
                source = pl.ds(pl.multiple_of(at * block, block), block)
                target = pl.ds(b * block, block)
                pltpu.make_async_copy(v_hbm.at[g, source], vbuf.at[i, target], vsem.at[i]).start()
                pltpu.make_async_copy(k_hbm.at[g, source], tiles.at[i, target], ksem.at[i]).start()
                scales[i, b] = ks_ref[g, at] * factor
            return 0

        lax.fori_loop(0, turns, fetch, 0)

    for g in range(heads):
        first, count, turns, start = spans[g]

        def turn(t, _, g=g, first=first, count=count, start=start):
            i = start + t
            some = pl.ds(0, keys)
            pltpu.make_async_copy(v_hbm.at[g, some], vbuf.at[i], vsem.at[i]).wait()
            for b in range(0, PER_TILE, LANES // block):
                rows = []
                for c in range(b, b + LANES // block):
                    slot = t * PER_TILE + c
                    at = sel_ref[g, first + jnp.minimum(slot, count - 1)] - base
                    scale = jnp.where(slot < count, vs_ref[g, at], 0.0)
                    rows.append(vbuf[i, c * block : (c + 1) * block, :].astype(jnp.float32) * scale)
                key_at = lax.broadcasted_iota(jnp.int32, (PACK, LANES), 1) + (t * keys + b * block)
                live = jnp.where(key_at < count * block, 1.0, 0.0).astype(jnp.bfloat16)
                at = keys + b * block // LANES * (width + PACK)
                tiles[i, at : at + width, :] = jnp.concatenate(rows, axis=0).T.astype(jnp.bfloat16)
                tiles[i, at + width : at + width + PACK, :] = live
            pltpu.make_async_copy(k_hbm.at[g, some], tiles.at[i, some], ksem.at[i]).wait()
            return 0

        lax.fori_loop(0, turns, turn, 0)


def collect(where, selection, key_scale, value_scale, k, v):
    heads, _, width = k.shape
    local = key_scale.shape[1]
    block = k.shape[1] // local
    keys = PER_TILE * block
    most = -(-min(MOST, local) // PER_TILE) * heads
    height = keys + keys // LANES * (width + PACK)
    return pl.pallas_call(
        functools.partial(collect_kernel, block, local),
        out_shape=[
            jax.ShapeDtypeStruct((most, height, width), jnp.bfloat16),
            jax.ShapeDtypeStruct((heads + 1,), jnp.int32),
            jax.ShapeDtypeStruct((most, PER_TILE), jnp.float32),
        ],
        in_specs=[SMEM, SMEM, SMEM, SMEM, HBM, HBM],
        out_specs=[VMEM, SMEM, SMEM],
        scratch_shapes=[
            pltpu.VMEM((most, keys, width), jnp.bfloat16),
            pltpu.SemaphoreType.DMA((most,)),
            pltpu.SemaphoreType.DMA((most,)),
        ],
        compiler_params=pltpu.CompilerParams(vmem_limit_bytes=58 << 20),
        cost_estimate=pl.CostEstimate(flops=0, bytes_accessed=6 << 20, transcendentals=0),
    )(where, selection, key_scale, value_scale, k, v)


def attend_kernel(cfg, where_ref, table, scales, q_ref, tiles, *rest):
    heads, group, owners, block = cfg
    msgs = rest[:owners]
    acc, m_scr, lse_scr = rest[owners:]
    keys = PER_TILE * block
    width = tiles.shape[-1]
    rows = acc.shape[2]
    low, high = table[heads[0]], table[heads[-1] + 1]

    def query(g):
        return q_ref[:, pl.ds(pl.multiple_of(g * group, group), group), :].reshape(rows, width)

    def score(k, q):
        return lax.dot_general(k, q, (((1,), (1,)), ((), ())), preferred_element_type=jnp.float32)

    def head_of(i):
        g = jnp.int32(heads[0])
        for h in heads[1:]:
            g = g + (i >= table[h]).astype(jnp.int32)
        return g

    def scaled(i, q):
        s = score(tiles[i, :keys, :], q)
        return [s[b * block : (b + 1) * block] * scales[i, b] for b in range(PER_TILE)]

    def values(i):
        step = width + PACK
        parts = [tiles[i, keys + c * step : keys + (c + 1) * step, :] for c in range(keys // LANES)]
        return jnp.concatenate(parts, axis=1)

    def quick(i, _):
        g = head_of(i)
        at = g - heads[0]
        m = m_scr[at]
        weights = [jnp.exp2(x - m).astype(jnp.bfloat16) for x in scaled(i, query(g))]
        acc[at] += jnp.dot(values(i), jnp.concatenate(weights, axis=0), preferred_element_type=jnp.float32)
        return 0

    def careful(i, _):
        g = head_of(i)
        at = g - heads[0]
        s = scaled(i, query(g))
        old = m_scr[at]
        new = jnp.maximum(old, jnp.max(functools.reduce(jnp.maximum, s), axis=0, keepdims=True))
        weights = jnp.concatenate([jnp.exp2(x - new).astype(jnp.bfloat16) for x in s], axis=0)
        acc[at] = acc[at] * jnp.exp2(old - new) + jnp.dot(
            values(i), weights, preferred_element_type=jnp.float32
        )
        m_scr[at] = new
        return 0

    acc[...] = jnp.zeros_like(acc)
    for n, g in enumerate(heads):
        first = table[g]
        q = q_ref[:, g * group : (g + 1) * group, :].reshape(rows, width)
        m_scr[n] = jnp.max(score(tiles[first, :block, :], q), axis=0, keepdims=True) * scales[first, 0]
    lax.fori_loop(low, high, quick, 0)

    @pl.when(jnp.logical_not(jnp.max(acc[:, width : width + 1, :]) < SAFE))
    def _():
        acc[...] = jnp.zeros_like(acc)
        m_scr[...] = jnp.full_like(m_scr, NEG)
        lax.fori_loop(low, high, careful, 0)

    blocks = rows // owners // LANES
    size = section(blocks, width)
    for d in range(owners):
        x = where_ref[1] ^ d
        for n in range(len(heads)):
            for b in range(blocks):
                at = pl.ds(pl.multiple_of((x * blocks + b) * LANES, LANES), LANES)
                total = acc[n, width : width + 1, at]
                row = n * size + b * width
                msgs[d][row : row + width, :] = (acc[n, :width, at] / total).astype(jnp.bfloat16)
                lse_scr[b : b + 1, :] = m_scr[n, :, at] + jnp.log2(total)
            put_level(msgs[d], lse_scr[...], n * size + blocks * width)


def section(blocks, width):
    return blocks * width + PARTS * PACK


def put_level(msg_ref, level, at):
    for i in range(PARTS):
        part = level.astype(jnp.bfloat16)
        msg_ref[at + i * PACK : at + i * PACK + level.shape[0], :] = part
        level = level - part.astype(jnp.float32)


def get_level(msg_ref, at):
    parts = [msg_ref[at + i * PACK : at + i * PACK + 8, :].astype(jnp.float32) for i in range(PARTS)]
    return functools.reduce(jnp.add, parts)


def merge_weights(refs, at):
    levels = [get_level(ref, at) for ref in refs]
    peak = functools.reduce(jnp.maximum, levels)
    shares = [jnp.exp2(level - peak) for level in levels]
    whole = functools.reduce(jnp.add, shares)
    return [share / whole for share in shares], peak + jnp.log2(whole)


def merged(refs, shares, row, b, width):
    values = [ref[row : row + width, :].astype(jnp.float32) * share[b : b + 1] for ref, share in zip(refs, shares)]
    return functools.reduce(jnp.add, values)


def merge_kernel(blocks, width, *refs):
    out = refs[-1]
    ins = refs[:-1]
    size = section(blocks, width)
    for n in range(out.shape[0] // size):
        shares, level = merge_weights(ins, n * size + blocks * width)
        for b in range(blocks):
            row = n * size + b * width
            out[row : row + width, :] = merged(ins, shares, row, b, width).astype(jnp.bfloat16)
        put_level(out, level, n * size + blocks * width)


def merge(msgs, blocks, width):
    return pl.pallas_call(
        functools.partial(merge_kernel, blocks, width),
        out_shape=jax.ShapeDtypeStruct(msgs[0].shape, msgs[0].dtype),
        in_specs=[VMEM] * len(msgs),
        out_specs=VMEM,
        compiler_params=pltpu.CompilerParams(vmem_limit_bytes=4 << 20),
        cost_estimate=pl.CostEstimate(flops=msgs[0].size * 4, bytes_accessed=msgs[0].size * 6, transcendentals=0),
    )(*msgs)


def finish_kernel(units, group, blocks, width, pick_ref, *refs):
    out, held, sems = refs[-3:]
    size = section(blocks, width)
    stages = 1 + max(k for k, _, _ in units)
    for stage in range(stages):

        @pl.when(pick_ref[0] == stage)
        def _(stage=stage):
            at = 0
            copies = []
            for k, heads, many in units:
                if k == stage:
                    for n, g in enumerate(heads):
                        for i in range(many):
                            source = refs[at + i].at[pl.ds(n * size, size)]
                            copies.append(pltpu.make_async_copy(source, held.at[g, i], sems.at[g, i]))
                at += many
            for copy in copies:
                copy.start()
            for copy in copies:
                copy.wait()

    tokens = LANES // group
    for g in range(held.shape[0]):
        ins = [held.at[g, i] for i in range(held.shape[1])]
        shares, _ = merge_weights(ins, blocks * width)
        for b in range(blocks):
            value = merged(ins, shares, b * width, b, width)
            turned = value.T.astype(jnp.bfloat16).reshape(tokens, group, width)
            out[b * tokens : (b + 1) * tokens, g * group : (g + 1) * group, :] = turned


def finish(pick, units, heads, group, blocks, width):
    many = len(units[0][2])
    msgs = [msg for _, _, msgs in units for msg in msgs]
    shape = tuple((k, hs, len(ms)) for k, hs, ms in units)
    return pl.pallas_call(
        functools.partial(finish_kernel, shape, group, blocks, width),
        out_shape=jax.ShapeDtypeStruct((blocks * LANES // group, heads * group, width), jnp.bfloat16),
        in_specs=[SMEM] + [HBM] * len(msgs),
        out_specs=VMEM,
        scratch_shapes=[
            pltpu.VMEM((heads, many, section(blocks, width), width), jnp.bfloat16),
            pltpu.SemaphoreType.DMA((heads, many)),
        ],
        compiler_params=pltpu.CompilerParams(vmem_limit_bytes=8 << 20),
    )(pick, *msgs)


def attend(where, table, scales, q, tiles, heads, group, owners, block):
    width = q.shape[2]
    rows = q.shape[0] * group
    blocks = rows // owners // LANES
    message = jax.ShapeDtypeStruct((len(heads) * section(blocks, width), width), jnp.bfloat16)
    likely = len(heads) * rows * 3 * PER_TILE * block
    return pl.pallas_call(
        functools.partial(attend_kernel, (heads, group, owners, block)),
        out_shape=[message] * owners,
        in_specs=[SMEM, SMEM, SMEM, VMEM, VMEM],
        out_specs=[VMEM] * owners,
        scratch_shapes=[
            pltpu.VMEM((len(heads), width + PACK, rows), jnp.float32),
            pltpu.VMEM((len(heads), 1, rows), jnp.float32),
            pltpu.VMEM((8, LANES), jnp.float32),
        ],
        compiler_params=pltpu.CompilerParams(vmem_limit_bytes=16 << 20),
        cost_estimate=pl.CostEstimate(flops=4 * likely * width, bytes_accessed=4 << 20, transcendentals=likely),
    )(where, table, scales, q, tiles)


def plan_units(head_size, heads):
    units = [(k, tuple(range(heads))) for k in range(head_size - 1)]
    return units + [(head_size - 1, (g,)) for g in range(heads)]


def on_device(ctx_size, head_size, queries, keys, values, key_block_scale, value_block_scale, selection):
    heads, _, width = keys.shape
    local = key_block_scale.shape[1]
    block = keys.shape[1] // local
    mine = queries.shape[1] // head_size
    group = mine // heads
    owners = ctx_size // head_size
    ctx = lax.axis_index("ctx")
    head = lax.axis_index("head")
    place, owner = ctx // owners, ctx % owners
    where = jnp.stack([ctx * local, owner]).astype(jnp.int32)
    blocks = queries.shape[0] * group // owners // LANES

    def part(k):
        return lax.dynamic_slice_in_dim(queries, (head ^ k) * mine, mine, axis=1)

    def swap(k):
        return lax.ppermute(part(k), "head", [(i, i ^ k) for i in range(head_size)])

    chunks = [part(0)] + [swap(k) for k in range(1, head_size)]
    tiles, table, scales = collect(where, selection, key_block_scale, value_block_scale, keys, values)

    def index(c, h):
        return c * head_size + h

    units = []
    for k, hs in plan_units(head_size, heads):
        msgs = attend(where, table, scales, chunks[k], tiles, hs, group, owners, block)
        got = [
            lax.ppermute(msgs[d], "ctx", [(c, c ^ d) for c in range(ctx_size)]) for d in range(1, owners)
        ]
        held = merge([msgs[0]] + got, blocks, width)
        far = [held]
        for apart in range(1, head_size):
            routes = []
            for c in range(ctx_size):
                for h in range(head_size):
                    if (c // owners) ^ h ^ k == apart:
                        routes.append((index(c, h), index(c ^ (apart * owners), h)))
            far.append(lax.ppermute(held, ("ctx", "head"), routes))
        units.append((k, hs, far))
    pick = (place ^ head).astype(jnp.int32).reshape(1)
    return finish(pick, units, heads, group, blocks, width)


def solution(mesh):
    ctx_size, head_size = mesh.shape["ctx"], mesh.shape["head"]

    def body(*args):
        return on_device(ctx_size, head_size, *args)

    return jax.shard_map(
        body,
        mesh=mesh,
        in_specs=(
            P("head", None, None),
            P("head", "ctx", None),
            P("head", "ctx", None),
            P("head", "ctx"),
            P("head", "ctx"),
            P("head", None),
        ),
        out_specs=P("ctx", "head", None),
        check_vma=False,
    )
```

time: 504 us -> 127 us (0.25)
  other arithmetic: 155 us -> 0.61 us
  waiting for transfers between devices: 138 us -> 27.1 us
  local copies, waits for them, and re-layouts: 84.7 us -> 14.1 us
  matrix products: 65.3 us -> 0 us
  Pallas kernels: 0 us -> 64.9 us
  blocking collectives: 33 us -> 0 us
  starting transfers between devices: 3.68 us -> 18.9 us
  between operations: 14.9 us -> 0.43 us
  loops' own time: 5.71 us -> 0 us
    select_n x24 -> x0, other arithmetic: 121 us -> none  [the longest x8 80.1 us: advance(): jnp.repeat(value_scales[block_ids], BLK, total_repeat_length=per_turn * BLK)]
    reduce_scatter x1 -> x0, waiting for transfers between devices: 70.1 us -> none  [on_device(): lax.psum_scatter((summed * fading[..., None]).astype(jnp.bfloat16), 'ctx'...]
    dot_general x16 -> x0, matrix products: 65.3 us -> none  [the longest x8 53.1 us: advance(): jnp.dot(weights, value_rows, preferred_element_type=jnp.float32)]
    pallas_call x0 -> x12, Pallas kernels: none -> 64.9 us  [the longest x5 56.5 us: attend(): pl.pallas_call(functools.partial(attend_kernel, (heads, group, owners, bl...]
    gather x56 -> x0, local copies, waits for them, and re-layouts: 61.2 us -> none  [the longest x8 17.3 us: advance(): value_rows = value_blocks[block_ids].reshape(per_turn * BLK, HEAD_SIZE)]
    unnamed x3 -> x0, waiting for transfers between devices: 55.4 us -> none
    pmax x1 -> x0, blocking collectives: 33 us -> none  [on_device(): highest = lax.pmax(row_peak, 'ctx')]
    ppermute x0 -> x23, waiting for transfers between devices: none -> 27.1 us  [the longest x15 16 us: on_device(): far.append(lax.ppermute(held, ('ctx', 'head'), routes))]
  transfers between devices with their start and end apart: 3 -> 23, of which waited for: 3 -> 6; matrix products, arithmetic and copies ran while one was open for 3% -> 0% of each run, Pallas kernels for 0% -> 49%
where the time goes in v1:
time: 127 us; the launch traced here: 126 us
  Pallas kernels  64.9 us (51%)
  waiting for transfers between devices  27.1 us (21%)
  starting transfers between devices  18.9 us (15%)
  local copies, waits for them, and re-layouts  14.1 us (11%)
    pallas_call x5, Pallas kernels, attend(): pl.pallas_call(functools.partial(attend_kernel, (heads, group, owners, bl...  56.5 us
    ppermute x15, waiting for transfers between devices, on_device(): far.append(lax.ppermute(held, ('ctx', 'head'), routes))  16 us
    ppermute x15, starting transfers between devices, on_device(): far.append(lax.ppermute(held, ('ctx', 'head'), routes))  14.4 us
    unnamed x32, local copies, waits for them, and re-layouts  11.2 us
    ppermute x5, waiting for transfers between devices, on_device(): lax.ppermute(msgs[d], 'ctx', [(c, c ^ d) for c in range(ctx_size)])  11.2 us
    pallas_call x1, Pallas kernels, collect(): pl.pallas_call(functools.partial(collect_kernel, block, local), out_shape...  5.16 us
    dynamic_slice x1, local copies, waits for them, and re-layouts, part(): return lax.dynamic_slice_in_dim(queries, (head ^ k) * mine, mine, axis=1)  2.9 us
    pallas_call x1, Pallas kernels, finish(): pl.pallas_call(functools.partial(finish_kernel, shape, group, blocks, wid...  2.71 us
  transfers between devices with their start and end apart: 23, of which 6 were waited for; matrix products, arithmetic and copies ran while one was open for 0% of the time, Pallas kernels for 49%

profile of v1, /device:TPU:4, one launch (start us, length us, event | category | flops | bytes accessed | tf_op | source)
XLA Modules:
  0.0 126.1 jit_solution(15070230318849019502)
XLA Ops:
  0.0 2.9 %constant_dynamic-slice_fusion = (bf16[64,32,128]{2,1,0:T(8,128)(2,1)}, bf16[64,32,128]{2,1,0:T(8,128)(2,1)}, bf16[64,32,128]{2,1,0:T(8,128)(2,1)S(1)}, bf16[64,32,128]{2,1,0:T(8,128)(2,1)}) fusion(bf16[64,128,128]{2,1,0:T(8,128)(2,1)} %param.6, s32[]{:T(128)S(6)} %select_n.28, s32[]{:T(128)S(6)} %select_n.26, s32[]{:T(128)S(6)} %select_n.25, s32[]{:T(128)S(6)} %select_n.27), kind=kLoop, calls=%fused_computation | loop fusion | bytes 4194320 | tf_op jit(solution)/shard_map/dynamic_slice | solution.py:343
  2.9 2.1 %collective-permute-start.9 = (bf16[64,32,128]{2,1,0:T(8,128)(2,1)}, bf16[64,32,128]{2,1,0:T(8,128)(2,1)S(1)}, u32[]{:S(2)}, u32[]{:S(2)}) collective-permute-start(bf16[64,32,128]{2,1,0:T(8,128)(2,1)} %get-tuple-element.34), channel_id=1, source_target_pairs={{0,2},{1,3},{2,0},{3,1},{4,6},{5,7},{6,4},{7,5},{8,10},{9,11},{10,... | collective-permute-start | bytes 1572872 | tf_op jit(solution)/shard_map/ppermute | solution.py:346
  5.7 5.2 %shard_map.64 = (bf16[10,1088,128]{2,1,0:T(8,128)(2,1)}, s32[3]{0:T(128)}, f32[10,8]{1,0:T(8,128)}) custom-call(s32[2]{0:T(128)} %pad_add_fusion.where_ref, s32[2,128]{1,0:T(2,128)} %sel_ref.1, f32[2,128]{1,0:T(2,128)} %ks_ref.1, f32[2,128]{1,0:T(2,128)} %vs_ref.1, bf16[2,8192,128]{2,1,0:T(8,128)(2,1)} %k_hbm.1, bf16[2,8192,128]{2,1,0:T(8,128)(2,1)} %v_hbm.1), custom_call_target="tpu_custom_call" | custom-call | bytes 6291456 | tf_op jit(solution)/shard_map/pallas_call | solution.py:105
  10.8 1.8 %copy-done = bf16[10,1088,128]{2,1,0:T(8,128)(2,1)S(1)} copy-done((bf16[10,1088,128]{2,1,0:T(8,128)(2,1)S(1)}, bf16[10,1088,128]{2,1,0:T(8,128)(2,1)}, u32[]{:S(2)}) %copy-start) | copy-done | bytes 2785304
  14.0 13.8 %shard_map.65 = (bf16[1120,128]{1,0:T(8,128)(2,1)S(1)}, bf16[1120,128]{1,0:T(8,128)(2,1)S(1)}) custom-call(s32[2]{0:T(128)S(1)} %copy-done.14, s32[3]{0:T(128)S(1)} %copy-done.15, f32[10,8]{1,0:T(8,128)S(1)} %copy-done.13, bf16[64,32,128]{2,1,0:T(8,128)(2,1)S(1)} %get-tuple-element.33.q_ref, bf16[10,1088,128]{2,1,0:T(8,128)(2,1)S(1)} %copy-done), custom_call_target="tpu_custom_call" | custom-call | flops 1610612736 | bytes 4194304 | tf_op jit(solution)/shard_map/pallas_call | solution.py:309
  27.9 6.6 %collective-permute-done.refs_1_ = bf16[1120,128]{1,0:T(8,128)(2,1)S(1)} collective-permute-done((bf16[1120,128]{1,0:T(8,128)(2,1)S(1)}, bf16[1120,128]{1,0:T(8,128)(2,1)S(1)}, u32[]{:S(2)}, u32[]{:S(2)}) %collective-permute-start) | collective-permute-done | bytes 286752 | tf_op jit(solution)/shard_map/ppermute | solution.py:358
  35.4 1.3 %collective-permute-start.2 = (bf16[1120,128]{1,0:T(8,128)(2,1)S(1)}, bf16[1120,128]{1,0:T(8,128)(2,1)S(1)}, u32[]{:S(2)}, u32[]{:S(2)}) collective-permute-start(bf16[1120,128]{1,0:T(8,128)(2,1)S(1)} %shard_map.66.refs_0_), channel_id=1, source_target_pairs={{2,18},{6,22},{11,27},{15,31},{16,0},{20,4},{25,9},{29,13}} | collective-permute-start | bytes 860168 | tf_op jit(solution)/shard_map/ppermute | solution.py:368
  37.4 9.0 %shard_map.73 = (bf16[560,128]{1,0:T(8,128)(2,1)S(1)}, bf16[560,128]{1,0:T(8,128)(2,1)S(1)}) custom-call(s32[2]{0:T(128)S(1)} %copy-done.14, s32[3]{0:T(128)S(1)} %copy-done.15, f32[10,8]{1,0:T(8,128)S(1)} %copy-done.13, bf16[64,32,128]{2,1,0:T(8,128)(2,1)S(1)} %collective-permute-done.14.q_ref, bf16[10,1088,128]{2,1,0:T(8,128)(2,1)S(1)} %copy-done), custom_call_target="tpu_custom_call" | custom-call | flops 805306368 | bytes 4194304 | tf_op jit(solution)/shard_map/pallas_call | solution.py:309
  46.5 13.8 %shard_map.67 = (bf16[1120,128]{1,0:T(8,128)(2,1)S(1)}, bf16[1120,128]{1,0:T(8,128)(2,1)S(1)}) custom-call(s32[2]{0:T(128)S(1)} %copy-done.14, s32[3]{0:T(128)S(1)} %copy-done.15, f32[10,8]{1,0:T(8,128)S(1)} %copy-done.13, bf16[64,32,128]{2,1,0:T(8,128)(2,1)S(1)} %collective-permute-done.4.q_ref, bf16[10,1088,128]{2,1,0:T(8,128)(2,1)S(1)} %copy-done), custom_call_target="tpu_custom_call" | custom-call | flops 1610612736 | bytes 4194304 | tf_op jit(solution)/shard_map/pallas_call | solution.py:309
  60.4 13.8 %shard_map.69 = (bf16[1120,128]{1,0:T(8,128)(2,1)S(1)}, bf16[1120,128]{1,0:T(8,128)(2,1)S(1)}) custom-call(s32[2]{0:T(128)S(1)} %copy-done.14, s32[3]{0:T(128)S(1)} %copy-done.15, f32[10,8]{1,0:T(8,128)S(1)} %copy-done.13, bf16[64,32,128]{2,1,0:T(8,128)(2,1)S(1)} %collective-permute-done.9.q_ref, bf16[10,1088,128]{2,1,0:T(8,128)(2,1)S(1)} %copy-done), custom_call_target="tpu_custom_call" | custom-call | flops 1610612736 | bytes 4194304 | tf_op jit(solution)/shard_map/pallas_call | solution.py:309
  74.3 5.9 %shard_map.71 = (bf16[560,128]{1,0:T(8,128)(2,1)S(1)}, bf16[560,128]{1,0:T(8,128)(2,1)S(1)}) custom-call(s32[2]{0:T(128)S(1)} %copy-done.14, s32[3]{0:T(128)S(1)} %copy-done.15, f32[10,8]{1,0:T(8,128)S(1)} %copy-done.13, bf16[64,32,128]{2,1,0:T(8,128)(2,1)S(1)} %collective-permute-done.14.q_ref, bf16[10,1088,128]{2,1,0:T(8,128)(2,1)S(1)} %copy-done), custom_call_target="tpu_custom_call" | custom-call | flops 805306368 | bytes 4194304 | tf_op jit(solution)/shard_map/pallas_call | solution.py:309
  80.3 2.0 %collective-permute-start.15 = (bf16[560,128]{1,0:T(8,128)(2,1)S(1)}, bf16[560,128]{1,0:T(8,128)(2,1)S(1)}, u32[]{:S(2)}, u32[]{:S(2)}) collective-permute-start(bf16[560,128]{1,0:T(8,128)(2,1)S(1)} %get-tuple-element.28), channel_id=1, source_target_pairs={{0,4},{4,0},{8,12},{12,8},{16,20},{20,16},{24,28},{28,24},{1,5},{5... | collective-permute-start | bytes 430088 | tf_op jit(solution)/shard_map/ppermute | solution.py:358
  83.9 4.5 %collective-permute-done.15.refs_1_ = bf16[560,128]{1,0:T(8,128)(2,1)S(1)} collective-permute-done((bf16[560,128]{1,0:T(8,128)(2,1)S(1)}, bf16[560,128]{1,0:T(8,128)(2,1)S(1)}, u32[]{:S(2)}, u32[]{:S(2)}) %collective-permute-start.15) | collective-permute-done | bytes 143392 | tf_op jit(solution)/shard_map/ppermute | solution.py:358
  88.4 1.3 %collective-permute-start.8 = (bf16[1120,128]{1,0:T(8,128)(2,1)S(1)}, bf16[1120,128]{1,0:T(8,128)(2,1)S(1)}, u32[]{:S(2)}, u32[]{:S(2)}) collective-permute-start(bf16[1120,128]{1,0:T(8,128)(2,1)S(1)} %shard_map.68.refs_4_), channel_id=1, source_target_pairs={{2,26},{6,30},{11,19},{15,23},{16,8},{20,12},{25,1},{29,5}} | collective-permute-start | bytes 860168 | tf_op jit(solution)/shard_map/ppermute | solution.py:368
  89.8 1.3 %collective-permute-start.20 = (bf16[560,128]{1,0:T(8,128)(2,1)S(1)}, bf16[560,128]{1,0:T(8,128)(2,1)S(1)}, u32[]{:S(2)}, u32[]{:S(2)}) collective-permute-start(bf16[560,128]{1,0:T(8,128)(2,1)S(1)} %shard_map.74.refs_16_), channel_id=1, source_target_pairs={{2,10},{6,14},{11,3},{15,7},{16,24},{20,28},{25,17},{29,21}} | collective-permute-start | bytes 430088 | tf_op jit(solution)/shard_map/ppermute | solution.py:368
  92.5 1.3 %collective-permute-start.16 = (bf16[560,128]{1,0:T(8,128)(2,1)S(1)}, bf16[560,128]{1,0:T(8,128)(2,1)S(1)}, u32[]{:S(2)}, u32[]{:S(2)}) collective-permute-start(bf16[560,128]{1,0:T(8,128)(2,1)S(1)} %shard_map.72.refs_12_), channel_id=1, source_target_pairs={{2,10},{6,14},{11,3},{15,7},{16,24},{20,28},{25,17},{29,21}} | collective-permute-start | bytes 430088 | tf_op jit(solution)/shard_map/ppermute | solution.py:368
  94.0 4.0 %collective-permute-done.20.refs_17_ = bf16[560,128]{1,0:T(8,128)(2,1)S(1)} collective-permute-done((bf16[560,128]{1,0:T(8,128)(2,1)S(1)}, bf16[560,128]{1,0:T(8,128)(2,1)S(1)}, u32[]{:S(2)}, u32[]{:S(2)}) %collective-permute-start.20) | collective-permute-done | bytes 143392 | tf_op jit(solution)/shard_map/ppermute | solution.py:368
  101.3 1.3 %collective-permute-start.13 = (bf16[1120,128]{1,0:T(8,128)(2,1)S(1)}, bf16[1120,128]{1,0:T(8,128)(2,1)S(1)}, u32[]{:S(2)}, u32[]{:S(2)}) collective-permute-start(bf16[1120,128]{1,0:T(8,128)(2,1)S(1)} %shard_map.70.refs_8_), channel_id=1, source_target_pairs={{1,25},{5,29},{8,16},{12,20},{19,11},{23,15},{26,2},{30,6}} | collective-permute-start | bytes 860168 | tf_op jit(solution)/shard_map/ppermute | solution.py:368
  103.3 1.3 %collective-permute-start.12 = (bf16[1120,128]{1,0:T(8,128)(2,1)S(1)}, bf16[1120,128]{1,0:T(8,128)(2,1)S(1)}, u32[]{:S(2)}, u32[]{:S(2)}) collective-permute-start(bf16[1120,128]{1,0:T(8,128)(2,1)S(1)} %shard_map.70.refs_8_), channel_id=1, source_target_pairs={{0,16},{4,20},{9,25},{13,29},{18,2},{22,6},{27,11},{31,15}} | collective-permute-start | bytes 860168 | tf_op jit(solution)/shard_map/ppermute | solution.py:368
  104.6 1.3 %collective-permute-start.11 = (bf16[1120,128]{1,0:T(8,128)(2,1)S(1)}, bf16[1120,128]{1,0:T(8,128)(2,1)}, u32[]{:S(2)}, u32[]{:S(2)}) collective-permute-start(bf16[1120,128]{1,0:T(8,128)(2,1)S(1)} %shard_map.70.refs_8_), channel_id=1, source_target_pairs={{3,11},{7,15},{10,2},{14,6},{17,25},{21,29},{24,16},{28,20}} | collective-permute-start | bytes 860168 | tf_op jit(solution)/shard_map/ppermute | solution.py:368
  106.0 5.9 %collective-permute-done.13.refs_11_ = bf16[1120,128]{1,0:T(8,128)(2,1)S(1)} collective-permute-done((bf16[1120,128]{1,0:T(8,128)(2,1)S(1)}, bf16[1120,128]{1,0:T(8,128)(2,1)S(1)}, u32[]{:S(2)}, u32[]{:S(2)}) %collective-permute-start.13) | collective-permute-done | bytes 286752 | tf_op jit(solution)/shard_map/ppermute | solution.py:368
  111.9 3.0 %collective-permute-done.12.refs_10_ = bf16[1120,128]{1,0:T(8,128)(2,1)S(1)} collective-permute-done((bf16[1120,128]{1,0:T(8,128)(2,1)S(1)}, bf16[1120,128]{1,0:T(8,128)(2,1)S(1)}, u32[]{:S(2)}, u32[]{:S(2)}) %collective-permute-start.12) | collective-permute-done | bytes 286752 | tf_op jit(solution)/shard_map/ppermute | solution.py:368
  114.8 3.1 %collective-permute-done.11.refs_9_ = bf16[1120,128]{1,0:T(8,128)(2,1)} collective-permute-done((bf16[1120,128]{1,0:T(8,128)(2,1)S(1)}, bf16[1120,128]{1,0:T(8,128)(2,1)}, u32[]{:S(2)}, u32[]{:S(2)}) %collective-permute-start.11) | collective-permute-done | bytes 286752 | tf_op jit(solution)/shard_map/ppermute | solution.py:368
  123.4 2.7 %shard_map.75 = bf16[32,32,128]{2,1,0:T(8,128)(2,1)} custom-call(s32[1]{0:T(128)} %bitcast.pick_ref, bf16[1120,128]{1,0:T(8,128)(2,1)S(1)} %shard_map.66.refs_0_, bf16[1120,128]{1,0:T(8,128)(2,1)S(1)} %collective-permute-done.1.refs_1_, bf16[1120,128]{1,0:T(8,128)(2,1)S(1)} %collective-permute-done.2.refs_2_, ...), custom_call_target="tpu_custom_call" | custom-call | tf_op jit(solution)/shard_map/pallas_call | solution.py:290
  (68 shorter events, 16.3 us)
Async XLA Ops:
  2.9 33.8 %collective-permute-start.14 = (bf16[64,32,128]{2,1,0:T(8,128)(2,1)}, bf16[64,32,128]{2,1,0:T(8,128)(2,1)S(1)}, u32[]{:S(2)}, u32[]{:S(2)}) collective-permute-start(bf16[64,32,128]{2,1,0:T(8,128)(2,1)} %get-tuple-element.31), channel_id=1, source_target_pairs={{0,3},{1,2},{2,1},{3,0},{4,7},{5,6},{6,5},{7,4},{8,11},{9,10},{10,... | collective-permute-start | bytes 1572872 | tf_op jit(solution)/shard_map/ppermute | solution.py:346
  2.9 43.5 %collective-permute-start.4 = (bf16[64,32,128]{2,1,0:T(8,128)(2,1)}, bf16[64,32,128]{2,1,0:T(8,128)(2,1)S(1)}, u32[]{:S(2)}, u32[]{:S(2)}) collective-permute-start(bf16[64,32,128]{2,1,0:T(8,128)(2,1)} %get-tuple-element.32), channel_id=1, source_target_pairs={{0,1},{1,0},{2,3},{3,2},{4,5},{5,4},{6,7},{7,6},{8,9},{9,8},{10,11... | collective-permute-start | bytes 1572872 | tf_op jit(solution)/shard_map/ppermute | solution.py:346
  2.9 57.5 %collective-permute-start.9 = (bf16[64,32,128]{2,1,0:T(8,128)(2,1)}, bf16[64,32,128]{2,1,0:T(8,128)(2,1)S(1)}, u32[]{:S(2)}, u32[]{:S(2)}) collective-permute-start(bf16[64,32,128]{2,1,0:T(8,128)(2,1)} %get-tuple-element.34), channel_id=1, source_target_pairs={{0,2},{1,3},{2,0},{3,1},{4,6},{5,7},{6,4},{7,5},{8,10},{9,11},{10,... | collective-permute-start | bytes 1572872 | tf_op jit(solution)/shard_map/ppermute | solution.py:346
  27.8 6.7 %collective-permute-start = (bf16[1120,128]{1,0:T(8,128)(2,1)S(1)}, bf16[1120,128]{1,0:T(8,128)(2,1)S(1)}, u32[]{:S(2)}, u32[]{:S(2)}) collective-permute-start(bf16[1120,128]{1,0:T(8,128)(2,1)S(1)} %get-tuple-element.22), channel_id=1, source_target_pairs={{0,4},{4,0},{8,12},{12,8},{16,20},{20,16},{24,28},{28,24},{1,5},{5... | collective-permute-start | bytes 860168 | tf_op jit(solution)/shard_map/ppermute | solution.py:358
  34.7 45.5 %collective-permute-start.3 = (bf16[1120,128]{1,0:T(8,128)(2,1)S(1)}, bf16[1120,128]{1,0:T(8,128)(2,1)S(1)}, u32[]{:S(2)}, u32[]{:S(2)}) collective-permute-start(bf16[1120,128]{1,0:T(8,128)(2,1)S(1)} %shard_map.66.refs_0_), channel_id=1, source_target_pairs={{3,27},{7,31},{10,18},{14,22},{17,9},{21,13},{24,0},{28,4}} | collective-permute-start | bytes 860168 | tf_op jit(solution)/shard_map/ppermute | solution.py:368
  35.4 47.0 %collective-permute-start.2 = (bf16[1120,128]{1,0:T(8,128)(2,1)S(1)}, bf16[1120,128]{1,0:T(8,128)(2,1)S(1)}, u32[]{:S(2)}, u32[]{:S(2)}) collective-permute-start(bf16[1120,128]{1,0:T(8,128)(2,1)S(1)} %shard_map.66.refs_0_), channel_id=1, source_target_pairs={{2,18},{6,22},{11,27},{15,31},{16,0},{20,4},{25,9},{29,13}} | collective-permute-start | bytes 860168 | tf_op jit(solution)/shard_map/ppermute | solution.py:368
  36.7 53.1 %collective-permute-start.1 = (bf16[1120,128]{1,0:T(8,128)(2,1)S(1)}, bf16[1120,128]{1,0:T(8,128)(2,1)S(1)}, u32[]{:S(2)}, u32[]{:S(2)}) collective-permute-start(bf16[1120,128]{1,0:T(8,128)(2,1)S(1)} %shard_map.66.refs_0_), channel_id=1, source_target_pairs={{1,9},{5,13},{8,0},{12,4},{19,27},{23,31},{26,18},{30,22}} | collective-permute-start | bytes 860168 | tf_op jit(solution)/shard_map/ppermute | solution.py:368
  46.4 33.8 %collective-permute-start.19 = (bf16[560,128]{1,0:T(8,128)(2,1)S(1)}, bf16[560,128]{1,0:T(8,128)(2,1)S(1)}, u32[]{:S(2)}, u32[]{:S(2)}) collective-permute-start(bf16[560,128]{1,0:T(8,128)(2,1)S(1)} %get-tuple-element.30), channel_id=1, source_target_pairs={{0,4},{4,0},{8,12},{12,8},{16,20},{20,16},{24,28},{28,24},{1,5},{5... | collective-permute-start | bytes 430088 | tf_op jit(solution)/shard_map/ppermute | solution.py:358
  60.4 22.7 %collective-permute-start.5 = (bf16[1120,128]{1,0:T(8,128)(2,1)S(1)}, bf16[1120,128]{1,0:T(8,128)(2,1)S(1)}, u32[]{:S(2)}, u32[]{:S(2)}) collective-permute-start(bf16[1120,128]{1,0:T(8,128)(2,1)S(1)} %get-tuple-element.24), channel_id=1, source_target_pairs={{0,4},{4,0},{8,12},{12,8},{16,20},{20,16},{24,28},{28,24},{1,5},{5... | collective-permute-start | bytes 860168 | tf_op jit(solution)/shard_map/ppermute | solution.py:358
  80.2 12.3 %collective-permute-start.10 = (bf16[1120,128]{1,0:T(8,128)(2,1)S(1)}, bf16[1120,128]{1,0:T(8,128)(2,1)S(1)}, u32[]{:S(2)}, u32[]{:S(2)}) collective-permute-start(bf16[1120,128]{1,0:T(8,128)(2,1)S(1)} %get-tuple-element.26), channel_id=1, source_target_pairs={{0,4},{4,0},{8,12},{12,8},{16,20},{20,16},{24,28},{28,24},{1,5},{5... | collective-permute-start | bytes 860168 | tf_op jit(solution)/shard_map/ppermute | solution.py:358
  80.3 8.1 %collective-permute-start.15 = (bf16[560,128]{1,0:T(8,128)(2,1)S(1)}, bf16[560,128]{1,0:T(8,128)(2,1)S(1)}, u32[]{:S(2)}, u32[]{:S(2)}) collective-permute-start(bf16[560,128]{1,0:T(8,128)(2,1)S(1)} %get-tuple-element.28), channel_id=1, source_target_pairs={{0,4},{4,0},{8,12},{12,8},{16,20},{20,16},{24,28},{28,24},{1,5},{5... | collective-permute-start | bytes 430088 | tf_op jit(solution)/shard_map/ppermute | solution.py:358
  82.4 8.8 %collective-permute-start.22 = (bf16[560,128]{1,0:T(8,128)(2,1)S(1)}, bf16[560,128]{1,0:T(8,128)(2,1)S(1)}, u32[]{:S(2)}, u32[]{:S(2)}) collective-permute-start(bf16[560,128]{1,0:T(8,128)(2,1)S(1)} %shard_map.74.refs_16_), channel_id=1, source_target_pairs={{0,24},{4,28},{9,17},{13,21},{18,10},{22,14},{27,3},{31,7}} | collective-permute-start | bytes 430088 | tf_op jit(solution)/shard_map/ppermute | solution.py:368
  83.1 8.8 %collective-permute-start.21 = (bf16[560,128]{1,0:T(8,128)(2,1)S(1)}, bf16[560,128]{1,0:T(8,128)(2,1)S(1)}, u32[]{:S(2)}, u32[]{:S(2)}) collective-permute-start(bf16[560,128]{1,0:T(8,128)(2,1)S(1)} %shard_map.74.refs_16_), channel_id=1, source_target_pairs={{1,17},{5,21},{8,24},{12,28},{19,3},{23,7},{26,10},{30,14}} | collective-permute-start | bytes 430088 | tf_op jit(solution)/shard_map/ppermute | solution.py:368
  88.4 16.2 %collective-permute-start.8 = (bf16[1120,128]{1,0:T(8,128)(2,1)S(1)}, bf16[1120,128]{1,0:T(8,128)(2,1)S(1)}, u32[]{:S(2)}, u32[]{:S(2)}) collective-permute-start(bf16[1120,128]{1,0:T(8,128)(2,1)S(1)} %shard_map.68.refs_4_), channel_id=1, source_target_pairs={{2,26},{6,30},{11,19},{15,23},{16,8},{20,12},{25,1},{29,5}} | collective-permute-start | bytes 860168 | tf_op jit(solution)/shard_map/ppermute | solution.py:368
  89.8 8.1 %collective-permute-start.20 = (bf16[560,128]{1,0:T(8,128)(2,1)S(1)}, bf16[560,128]{1,0:T(8,128)(2,1)S(1)}, u32[]{:S(2)}, u32[]{:S(2)}) collective-permute-start(bf16[560,128]{1,0:T(8,128)(2,1)S(1)} %shard_map.74.refs_16_), channel_id=1, source_target_pairs={{2,10},{6,14},{11,3},{15,7},{16,24},{20,28},{25,17},{29,21}} | collective-permute-start | bytes 430088 | tf_op jit(solution)/shard_map/ppermute | solution.py:368
  91.1 13.5 %copy-start.1 = (bf16[560,128]{1,0:T(8,128)(2,1)}, bf16[560,128]{1,0:T(8,128)(2,1)S(1)}, u32[]{:S(2)}) copy-start(bf16[560,128]{1,0:T(8,128)(2,1)S(1)} %collective-permute-done.22.refs_19_) | copy-start | bytes 430084
  91.1 8.2 %collective-permute-start.18 = (bf16[560,128]{1,0:T(8,128)(2,1)S(1)}, bf16[560,128]{1,0:T(8,128)(2,1)S(1)}, u32[]{:S(2)}, u32[]{:S(2)}) collective-permute-start(bf16[560,128]{1,0:T(8,128)(2,1)S(1)} %shard_map.72.refs_12_), channel_id=1, source_target_pairs={{0,24},{4,28},{9,17},{13,21},{18,10},{22,14},{27,3},{31,7}} | collective-permute-start | bytes 430088 | tf_op jit(solution)/shard_map/ppermute | solution.py:368
  91.8 8.8 %collective-permute-start.17 = (bf16[560,128]{1,0:T(8,128)(2,1)S(1)}, bf16[560,128]{1,0:T(8,128)(2,1)S(1)}, u32[]{:S(2)}, u32[]{:S(2)}) collective-permute-start(bf16[560,128]{1,0:T(8,128)(2,1)S(1)} %shard_map.72.refs_12_), channel_id=1, source_target_pairs={{1,17},{5,21},{8,24},{12,28},{19,3},{23,7},{26,10},{30,14}} | collective-permute-start | bytes 430088 | tf_op jit(solution)/shard_map/ppermute | solution.py:368
  92.5 10.1 %collective-permute-start.16 = (bf16[560,128]{1,0:T(8,128)(2,1)S(1)}, bf16[560,128]{1,0:T(8,128)(2,1)S(1)}, u32[]{:S(2)}, u32[]{:S(2)}) collective-permute-start(bf16[560,128]{1,0:T(8,128)(2,1)S(1)} %shard_map.72.refs_12_), channel_id=1, source_target_pairs={{2,10},{6,14},{11,3},{15,7},{16,24},{20,28},{25,17},{29,21}} | collective-permute-start | bytes 430088 | tf_op jit(solution)/shard_map/ppermute | solution.py:368
  98.6 7.3 %collective-permute-start.7 = (bf16[1120,128]{1,0:T(8,128)(2,1)S(1)}, bf16[1120,128]{1,0:T(8,128)(2,1)S(1)}, u32[]{:S(2)}, u32[]{:S(2)}) collective-permute-start(bf16[1120,128]{1,0:T(8,128)(2,1)S(1)} %shard_map.68.refs_4_), channel_id=1, source_target_pairs={{3,19},{7,23},{10,26},{14,30},{17,1},{21,5},{24,8},{28,12}} | collective-permute-start | bytes 860168 | tf_op jit(solution)/shard_map/ppermute | solution.py:368
  100.0 6.0 %collective-permute-start.6 = (bf16[1120,128]{1,0:T(8,128)(2,1)S(1)}, bf16[1120,128]{1,0:T(8,128)(2,1)S(1)}, u32[]{:S(2)}, u32[]{:S(2)}) collective-permute-start(bf16[1120,128]{1,0:T(8,128)(2,1)S(1)} %shard_map.68.refs_4_), channel_id=1, source_target_pairs={{0,8},{4,12},{9,1},{13,5},{18,26},{22,30},{27,19},{31,23}} | collective-permute-start | bytes 860168 | tf_op jit(solution)/shard_map/ppermute | solution.py:368
  101.3 10.5 %collective-permute-start.13 = (bf16[1120,128]{1,0:T(8,128)(2,1)S(1)}, bf16[1120,128]{1,0:T(8,128)(2,1)S(1)}, u32[]{:S(2)}, u32[]{:S(2)}) collective-permute-start(bf16[1120,128]{1,0:T(8,128)(2,1)S(1)} %shard_map.70.refs_8_), channel_id=1, source_target_pairs={{1,25},{5,29},{8,16},{12,20},{19,11},{23,15},{26,2},{30,6}} | collective-permute-start | bytes 860168 | tf_op jit(solution)/shard_map/ppermute | solution.py:368
  103.3 11.5 %collective-permute-start.12 = (bf16[1120,128]{1,0:T(8,128)(2,1)S(1)}, bf16[1120,128]{1,0:T(8,128)(2,1)S(1)}, u32[]{:S(2)}, u32[]{:S(2)}) collective-permute-start(bf16[1120,128]{1,0:T(8,128)(2,1)S(1)} %shard_map.70.refs_8_), channel_id=1, source_target_pairs={{0,16},{4,20},{9,25},{13,29},{18,2},{22,6},{27,11},{31,15}} | collective-permute-start | bytes 860168 | tf_op jit(solution)/shard_map/ppermute | solution.py:368
  104.6 13.3 %collective-permute-start.11 = (bf16[1120,128]{1,0:T(8,128)(2,1)S(1)}, bf16[1120,128]{1,0:T(8,128)(2,1)}, u32[]{:S(2)}, u32[]{:S(2)}) collective-permute-start(bf16[1120,128]{1,0:T(8,128)(2,1)S(1)} %shard_map.70.refs_8_), channel_id=1, source_target_pairs={{3,11},{7,15},{10,2},{14,6},{17,25},{21,29},{24,16},{28,20}} | collective-permute-start | bytes 860168 | tf_op jit(solution)/shard_map/ppermute | solution.py:368
  (15 other events, 29.2 us)

commit v2 on v1

--- a/solution.py
+++ b/solution.py
@@ -22,6 +22,10 @@
 HBM = pl.BlockSpec(memory_space=pltpu.HBM)
 
 
+def keep_out(x):
+    return pltpu.with_memory_space_constraint(x, pltpu.HBM)
+
+
 def locate(sel_ref, g, bound):
     length = sel_ref.shape[1]
 
@@ -36,12 +40,12 @@
     return lax.fori_loop(0, length.bit_length(), halve, span)[0]
 
 
-def collect_kernel(block, local, where_ref, sel_ref, ks_ref, vs_ref, k_hbm, v_hbm, tiles, table, scales, vbuf, ksem, vsem):
+def collect_kernel(block, local, sel_ref, ks_ref, vs_ref, k_hbm, v_hbm, tiles, table, scales, vbuf, ksem, vsem):
     heads, _, width = k_hbm.shape
     most = (tiles.shape[0]) // heads
     keys = PER_TILE * block
     factor = math.log2(math.e) / math.sqrt(width)
-    base = where_ref[0]
+    base = lax.axis_index("ctx") * local
     spans = []
     start = jnp.int32(0)
     for g in range(heads):
@@ -95,7 +99,7 @@
         lax.fori_loop(0, turns, turn, 0)
 
 
-def collect(where, selection, key_scale, value_scale, k, v):
+def collect(selection, key_scale, value_scale, k, v):
     heads, _, width = k.shape
     local = key_scale.shape[1]
     block = k.shape[1] // local
@@ -109,19 +113,19 @@
             jax.ShapeDtypeStruct((heads + 1,), jnp.int32),
             jax.ShapeDtypeStruct((most, PER_TILE), jnp.float32),
         ],
-        in_specs=[SMEM, SMEM, SMEM, SMEM, HBM, HBM],
+        in_specs=[SMEM, SMEM, SMEM, HBM, HBM],
         out_specs=[VMEM, SMEM, SMEM],
         scratch_shapes=[
             pltpu.VMEM((most, keys, width), jnp.bfloat16),
             pltpu.SemaphoreType.DMA((most,)),
             pltpu.SemaphoreType.DMA((most,)),
         ],
-        compiler_params=pltpu.CompilerParams(vmem_limit_bytes=58 << 20),
+        compiler_params=pltpu.CompilerParams(vmem_limit_bytes=16 << 20),
         cost_estimate=pl.CostEstimate(flops=0, bytes_accessed=6 << 20, transcendentals=0),
-    )(where, selection, key_scale, value_scale, k, v)
-
-
-def attend_kernel(cfg, where_ref, table, scales, q_ref, tiles, *rest):
+    )(selection, key_scale, value_scale, k, v)
+
+
+def attend_kernel(cfg, table, scales, q_ref, tiles, *rest):
     heads, group, owners, block = cfg
     msgs = rest[:owners]
     acc, m_scr, lse_scr = rest[owners:]
@@ -188,7 +192,7 @@
     blocks = rows // owners // LANES
     size = section(blocks, width)
     for d in range(owners):
-        x = where_ref[1] ^ d
+        x = lax.rem(lax.axis_index("ctx"), owners) ^ d
         for n in range(len(heads)):
             for b in range(blocks):
                 at = pl.ds(pl.multiple_of((x * blocks + b) * LANES, LANES), LANES)
@@ -251,13 +255,60 @@
     )(*msgs)
 
 
-def finish_kernel(units, group, blocks, width, pick_ref, *refs):
+def part_kernel(group, q_hbm, *refs):
+    chunks, sems = refs[:-1], refs[-1]
+    copies = []
+    for k, chunk in enumerate(chunks):
+        at = pl.multiple_of((lax.axis_index("head") ^ k) * group, group)
+        copies.append(pltpu.make_async_copy(q_hbm.at[:, pl.ds(at, group), :], chunk, sems.at[k]))
+    for copy in copies:
+        copy.start()
+    for copy in copies:
+        copy.wait()
+
+
+def part(queries, many):
+    tokens, heads, width = queries.shape
+    return pl.pallas_call(
+        functools.partial(part_kernel, heads // many),
+        out_shape=[jax.ShapeDtypeStruct((tokens, heads // many, width), queries.dtype)] * many,
+        in_specs=[HBM],
+        out_specs=[VMEM] * many,
+        scratch_shapes=[pltpu.SemaphoreType.DMA((many,))],
+        compiler_params=pltpu.CompilerParams(vmem_limit_bytes=16 << 20),
+    )(queries)
+
+
+def pair_kernel(blocks, width, owners, *refs):
+    keep, send = refs[-2:]
+    low, high = refs[:owners], refs[owners : 2 * owners]
+    swapped = (lax.axis_index("ctx") // owners ^ lax.axis_index("head")) & 1
+    for flag, first, second in ((0, low, high), (1, high, low)):
+
+        @pl.when(swapped == flag)
+        def _(first=first, second=second):
+            merge_kernel(blocks, width, *first, keep)
+            merge_kernel(blocks, width, *second, send)
+
+
+def merge_pair(low, high, blocks, width):
+    return pl.pallas_call(
+        functools.partial(pair_kernel, blocks, width, len(low)),
+        out_shape=[jax.ShapeDtypeStruct(low[0].shape, low[0].dtype)] * 2,
+        in_specs=[VMEM] * (2 * len(low)),
+        out_specs=[VMEM] * 2,
+        compiler_params=pltpu.CompilerParams(vmem_limit_bytes=4 << 20),
+        cost_estimate=pl.CostEstimate(flops=low[0].size * 8, bytes_accessed=low[0].size * 12, transcendentals=0),
+    )(*low, *high)
+
+
+def finish_kernel(units, group, blocks, width, owners, *refs):
     out, held, sems = refs[-3:]
     size = section(blocks, width)
-    stages = 1 + max(k for k, _, _ in units)
-    for stage in range(stages):
-
-        @pl.when(pick_ref[0] == stage)
+    picked = (lax.axis_index("ctx") // owners ^ lax.axis_index("head")) // 2
+    for stage in range(1 + max(k for k, _, _ in units)):
+
+        @pl.when(picked == stage)
         def _(stage=stage):
             at = 0
             copies = []
@@ -283,24 +334,24 @@
             out[b * tokens : (b + 1) * tokens, g * group : (g + 1) * group, :] = turned
 
 
-def finish(pick, units, heads, group, blocks, width):
+def finish(units, heads, group, blocks, width, owners):
     many = len(units[0][2])
     msgs = [msg for _, _, msgs in units for msg in msgs]
     shape = tuple((k, hs, len(ms)) for k, hs, ms in units)
     return pl.pallas_call(
-        functools.partial(finish_kernel, shape, group, blocks, width),
+        functools.partial(finish_kernel, shape, group, blocks, width, owners),
         out_shape=jax.ShapeDtypeStruct((blocks * LANES // group, heads * group, width), jnp.bfloat16),
-        in_specs=[SMEM] + [HBM] * len(msgs),
+        in_specs=[HBM] * len(msgs),
         out_specs=VMEM,
         scratch_shapes=[
             pltpu.VMEM((heads, many, section(blocks, width), width), jnp.bfloat16),
             pltpu.SemaphoreType.DMA((heads, many)),
         ],
         compiler_params=pltpu.CompilerParams(vmem_limit_bytes=8 << 20),
-    )(pick, *msgs)
-
-
-def attend(where, table, scales, q, tiles, heads, group, owners, block):
+    )(*msgs)
+
+
+def attend(table, scales, q, tiles, heads, group, owners, block):
     width = q.shape[2]
     rows = q.shape[0] * group
     blocks = rows // owners // LANES
@@ -309,7 +360,7 @@
     return pl.pallas_call(
         functools.partial(attend_kernel, (heads, group, owners, block)),
         out_shape=[message] * owners,
-        in_specs=[SMEM, SMEM, SMEM, VMEM, VMEM],
+        in_specs=[SMEM, SMEM, VMEM, VMEM],
         out_specs=[VMEM] * owners,
         scratch_shapes=[
             pltpu.VMEM((len(heads), width + PACK, rows), jnp.float32),
@@ -318,57 +369,53 @@
         ],
         compiler_params=pltpu.CompilerParams(vmem_limit_bytes=16 << 20),
         cost_estimate=pl.CostEstimate(flops=4 * likely * width, bytes_accessed=4 << 20, transcendentals=likely),
-    )(where, table, scales, q, tiles)
+    )(table, scales, q, tiles)
 
 
 def plan_units(head_size, heads):
-    units = [(k, tuple(range(heads))) for k in range(head_size - 1)]
-    return units + [(head_size - 1, (g,)) for g in range(heads)]
+    pieces = [(p, tuple(range(heads))) for p in range(head_size // 2 - 1)]
+    return pieces + [(head_size // 2 - 1, (g,)) for g in range(heads)]
 
 
 def on_device(ctx_size, head_size, queries, keys, values, key_block_scale, value_block_scale, selection):
     heads, _, width = keys.shape
     local = key_block_scale.shape[1]
     block = keys.shape[1] // local
-    mine = queries.shape[1] // head_size
-    group = mine // heads
+    group = queries.shape[1] // head_size // heads
     owners = ctx_size // head_size
-    ctx = lax.axis_index("ctx")
-    head = lax.axis_index("head")
-    place, owner = ctx // owners, ctx % owners
-    where = jnp.stack([ctx * local, owner]).astype(jnp.int32)
     blocks = queries.shape[0] * group // owners // LANES
 
-    def part(k):
-        return lax.dynamic_slice_in_dim(queries, (head ^ k) * mine, mine, axis=1)
-
-    def swap(k):
-        return lax.ppermute(part(k), "head", [(i, i ^ k) for i in range(head_size)])
-
-    chunks = [part(0)] + [swap(k) for k in range(1, head_size)]
-    tiles, table, scales = collect(where, selection, key_block_scale, value_block_scale, keys, values)
+    chunks = list(part(keep_out(queries), head_size))
+    for k in range(1, head_size):
+        chunks[k] = lax.ppermute(chunks[k], "head", [(i, i ^ k) for i in range(head_size)])
+    tiles, table, scales = collect(*map(keep_out, (selection, key_block_scale, value_block_scale, keys, values)))
 
     def index(c, h):
         return c * head_size + h
 
     units = []
-    for k, hs in plan_units(head_size, heads):
-        msgs = attend(where, table, scales, chunks[k], tiles, hs, group, owners, block)
-        got = [
-            lax.ppermute(msgs[d], "ctx", [(c, c ^ d) for c in range(ctx_size)]) for d in range(1, owners)
-        ]
-        held = merge([msgs[0]] + got, blocks, width)
-        far = [held]
-        for apart in range(1, head_size):
+    for p, hs in plan_units(head_size, heads):
+        gathered = []
+        for k in (2 * p, 2 * p + 1):
+            msgs = attend(table, scales, chunks[k], tiles, hs, group, owners, block)
+            got = [
+                lax.ppermute(msgs[d], "ctx", [(c, c ^ d) for c in range(ctx_size)]) for d in range(1, owners)
+            ]
+            gathered.append([msgs[0]] + got)
+        held, sent = merge_pair(*gathered, blocks, width)
+        got = lax.ppermute(sent, "ctx", [(c, c ^ owners) for c in range(ctx_size)])
+        for bit in range(1, head_size.bit_length() - 1):
+            held = merge([held, got], blocks, width)
             routes = []
+            step = 1 << bit
             for c in range(ctx_size):
                 for h in range(head_size):
-                    if (c // owners) ^ h ^ k == apart:
-                        routes.append((index(c, h), index(c ^ (apart * owners), h)))
-            far.append(lax.ppermute(held, ("ctx", "head"), routes))
-        units.append((k, hs, far))
-    pick = (place ^ head).astype(jnp.int32).reshape(1)
-    return finish(pick, units, heads, group, blocks, width)
+                    apart = (c // owners ^ h ^ 2 * p) & (2 * step - 2)
+                    if apart == step:
+                        routes.append((index(c, h), index(c ^ (step * owners), h)))
+            got = lax.ppermute(held, ("ctx", "head"), routes)
+        units.append((p, hs, [held, got]))
+    return finish(units, heads, group, blocks, width, owners)
 
 
 def solution(mesh):

time: 127 us -> 90.1 us (0.71)
  local copies, waits for them, and re-layouts: 14.1 us -> 0 us
  starting transfers between devices: 18.9 us -> 6.43 us
  waiting for transfers between devices: 27.1 us -> 17.2 us
    unnamed x32 -> x0, local copies, waits for them, and re-layouts: 11.2 us -> none
    ppermute x18 -> x9, starting transfers between devices: 16.6 us -> 6.02 us  [the longest x3 3.89 us: on_device(): got = lax.ppermute(held, ('ctx', 'head'), routes)]
    ppermute x5 -> x6, waiting for transfers between devices: 11.2 us -> 4.81 us  [on_device(): lax.ppermute(msgs[d], 'ctx', [(c, c ^ d) for c in range(ctx_size)])]
    ppermute x18 -> x9, waiting for transfers between devices: 16 us -> 12.3 us  [the longest x3 8.9 us: on_device(): got = lax.ppermute(held, ('ctx', 'head'), routes)]
    dynamic_slice x1 -> x0, local copies, waits for them, and re-layouts: 2.9 us -> none  [part(): return lax.dynamic_slice_in_dim(queries, (head ^ k) * mine, mine, axis=1)]
    pallas_call x0 -> x4, Pallas kernels: none -> 2.19 us  [the longest x1 1.56 us: part(): pl.pallas_call(functools.partial(part_kernel, heads // many), out_shape=[...]
    ppermute x5 -> x6, starting transfers between devices: 2.29 us -> 0.42 us  [on_device(): lax.ppermute(msgs[d], 'ctx', [(c, c ^ d) for c in range(ctx_size)])]
    pallas_call x5 -> x6, Pallas kernels: 56.5 us -> 57.5 us  [attend(): pl.pallas_call(functools.partial(attend_kernel, (heads, group, owners, bl...]
  transfers between devices with their start and end apart: 23 -> 15, of which waited for: 6 -> 4; matrix products, arithmetic and copies ran while one was open for 0% -> 0% of each run, Pallas kernels for 49% -> 70%
where the time goes in v2:
time: 90.1 us; the launch traced here: 89.9 us
  Pallas kernels  66 us (73%)
  waiting for transfers between devices  17.2 us (19%)
  starting transfers between devices  6.43 us (7%)
    pallas_call x6, Pallas kernels, attend(): pl.pallas_call(functools.partial(attend_kernel, (heads, group, owners, bl...  57.5 us
    ppermute x3, waiting for transfers between devices, on_device(): got = lax.ppermute(held, ('ctx', 'head'), routes)  8.9 us
    ppermute x6, waiting for transfers between devices, on_device(): lax.ppermute(msgs[d], 'ctx', [(c, c ^ d) for c in range(ctx_size)])  4.81 us
    pallas_call x1, Pallas kernels, collect(): pl.pallas_call(functools.partial(collect_kernel, block, local), out_shape...  4.38 us
    ppermute x3, starting transfers between devices, on_device(): got = lax.ppermute(held, ('ctx', 'head'), routes)  3.89 us
    ppermute x3, waiting for transfers between devices, on_device(): got = lax.ppermute(sent, 'ctx', [(c, c ^ owners) for c in range(ctx_size)])  3.44 us
    ppermute x3, starting transfers between devices, on_device(): lax.ppermute(chunks[k], 'head', [(i, i ^ k) for i in range(head_size)])  1.91 us
  transfers between devices with their start and end apart: 15, of which 4 were waited for; matrix products, arithmetic and copies ran while one was open for 0% of the time, Pallas kernels for 70%

profile of v2, /device:TPU:4, one launch (start us, length us, event | category | flops | bytes accessed | tf_op | source)
XLA Modules:
  0.0 89.9 jit_solution(7359887284126746094)
XLA Ops:
  0.0 1.6 %shard_map.65 = (bf16[64,32,128]{2,1,0:T(8,128)(2,1)S(1)}, bf16[64,32,128]{2,1,0:T(8,128)(2,1)S(1)}, bf16[64,32,128]{2,1,0:T(8,128)(2,1)S(1)}, bf16[64,32,128]{2,1,0:T(8,128)(2,1)S(1)}) custom-call(bf16[64,128,128]{2,1,0:T(8,128)(2,1)} %q_hbm.1), custom_call_target="tpu_custom_call" | custom-call | tf_op jit(solution)/shard_map/pallas_call | solution.py:272
  1.6 0.1 collective-permute-start.5
  1.7 1.8 %collective-permute-start.7 = (bf16[64,32,128]{2,1,0:T(8,128)(2,1)S(1)}, bf16[64,32,128]{2,1,0:T(8,128)(2,1)S(1)}, u32[]{:S(2)}, u32[]{:S(2)}) collective-permute-start(bf16[64,32,128]{2,1,0:T(8,128)(2,1)S(1)} %get-tuple-element.44), channel_id=1, source_target_pairs={{0,3},{1,2},{2,1},{3,0},{4,7},{5,6},{6,5},{7,4},{8,11},{9,10},{10,... | collective-permute-start | bytes 1572872 | tf_op jit(solution)/shard_map/ppermute | solution.py:390
  3.5 4.4 %shard_map.64 = (bf16[10,1088,128]{2,1,0:T(8,128)(2,1)S(1)}, s32[3]{0:T(128)S(1)}, f32[10,8]{1,0:T(8,128)S(1)}) custom-call(s32[2,128]{1,0:T(2,128)} %sel_ref.1, f32[2,128]{1,0:T(2,128)} %ks_ref.1, f32[2,128]{1,0:T(2,128)} %vs_ref.1, bf16[2,8192,128]{2,1,0:T(8,128)(2,1)} %k_hbm.1, bf16[2,8192,128]{2,1,0:T(8,128)(2,1)} %v_hbm.1), custom_call_target="tpu_custom_call" | custom-call | bytes 6291456 | tf_op jit(solution)/shard_map/pallas_call | solution.py:109
  7.9 13.9 %shard_map.66 = (bf16[1120,128]{1,0:T(8,128)(2,1)S(1)}, bf16[1120,128]{1,0:T(8,128)(2,1)S(1)}) custom-call(s32[3]{0:T(128)S(1)} %get-tuple-element.30.table, f32[10,8]{1,0:T(8,128)S(1)} %get-tuple-element.31.scales, bf16[64,32,128]{2,1,0:T(8,128)(2,1)S(1)} %get-tuple-element.32.q_ref, bf16[10,1088,128]{2,1,0:T(8,128)(2,1)S(1)} %get-tuple-element.33.tiles), custom_call_target="tpu_custom_call" | custom-call | flops 1610612736 | bytes 4194304 | tf_op jit(solution)/shard_map/pallas_call | solution.py:360
  21.7 0.1 collective-permute-start
  21.8 13.9 %shard_map.67 = (bf16[1120,128]{1,0:T(8,128)(2,1)S(1)}, bf16[1120,128]{1,0:T(8,128)(2,1)S(1)}) custom-call(s32[3]{0:T(128)S(1)} %get-tuple-element.30.table, f32[10,8]{1,0:T(8,128)S(1)} %get-tuple-element.31.scales, bf16[64,32,128]{2,1,0:T(8,128)(2,1)S(1)} %collective-permute-done.1.q_ref, bf16[10,1088,128]{2,1,0:T(8,128)(2,1)S(1)} %get-tuple-element.33.tiles), custom_call_target="tpu_custom_call" | custom-call | flops 1610612736 | bytes 4194304 | tf_op jit(solution)/shard_map/pallas_call | solution.py:360
  35.8 5.9 %shard_map.70 = (bf16[560,128]{1,0:T(8,128)(2,1)S(1)}, bf16[560,128]{1,0:T(8,128)(2,1)S(1)}) custom-call(s32[3]{0:T(128)S(1)} %get-tuple-element.30.table, f32[10,8]{1,0:T(8,128)S(1)} %get-tuple-element.31.scales, bf16[64,32,128]{2,1,0:T(8,128)(2,1)S(1)} %collective-permute-done.5.q_ref, bf16[10,1088,128]{2,1,0:T(8,128)(2,1)S(1)} %get-tuple-element.33.tiles), custom_call_target="tpu_custom_call" | custom-call | flops 805306368 | bytes 4194304 | tf_op jit(solution)/shard_map/pallas_call | solution.py:360
  41.8 5.9 %shard_map.71 = (bf16[560,128]{1,0:T(8,128)(2,1)S(1)}, bf16[560,128]{1,0:T(8,128)(2,1)S(1)}) custom-call(s32[3]{0:T(128)S(1)} %get-tuple-element.30.table, f32[10,8]{1,0:T(8,128)S(1)} %get-tuple-element.31.scales, bf16[64,32,128]{2,1,0:T(8,128)(2,1)S(1)} %collective-permute-done.7.q_ref, bf16[10,1088,128]{2,1,0:T(8,128)(2,1)S(1)} %get-tuple-element.33.tiles), custom_call_target="tpu_custom_call" | custom-call | flops 805306368 | bytes 4194304 | tf_op jit(solution)/shard_map/pallas_call | solution.py:360
  47.7 0.3 shard_map.68
  48.1 9.0 %shard_map.74 = (bf16[560,128]{1,0:T(8,128)(2,1)S(1)}, bf16[560,128]{1,0:T(8,128)(2,1)S(1)}) custom-call(s32[3]{0:T(128)S(1)} %get-tuple-element.30.table, f32[10,8]{1,0:T(8,128)S(1)} %get-tuple-element.31.scales, bf16[64,32,128]{2,1,0:T(8,128)(2,1)S(1)} %collective-permute-done.5.q_ref, bf16[10,1088,128]{2,1,0:T(8,128)(2,1)S(1)} %get-tuple-element.33.tiles), custom_call_target="tpu_custom_call" | custom-call | flops 805306368 | bytes 4194304 | tf_op jit(solution)/shard_map/pallas_call | solution.py:360
  57.2 9.0 %shard_map.75 = (bf16[560,128]{1,0:T(8,128)(2,1)S(1)}, bf16[560,128]{1,0:T(8,128)(2,1)S(1)}) custom-call(s32[3]{0:T(128)S(1)} %get-tuple-element.30.table, f32[10,8]{1,0:T(8,128)S(1)} %get-tuple-element.31.scales, bf16[64,32,128]{2,1,0:T(8,128)(2,1)S(1)} %collective-permute-done.7.q_ref, bf16[10,1088,128]{2,1,0:T(8,128)(2,1)S(1)} %get-tuple-element.33.tiles), custom_call_target="tpu_custom_call" | custom-call | flops 805306368 | bytes 4194304 | tf_op jit(solution)/shard_map/pallas_call | solution.py:360
  66.3 0.2 shard_map.72
  66.6 4.8 %collective-permute-done.12.refs_3_ = bf16[560,128]{1,0:T(8,128)(2,1)S(1)} collective-permute-done((bf16[560,128]{1,0:T(8,128)(2,1)S(1)}, bf16[560,128]{1,0:T(8,128)(2,1)S(1)}, u32[]{:S(2)}, u32[]{:S(2)}) %collective-permute-start.12) | collective-permute-done | bytes 143392 | tf_op jit(solution)/shard_map/ppermute | solution.py:402
  71.4 0.1 shard_map.76
  71.6 0.1 shard_map.69.refs_0_
  71.8 1.3 %collective-permute-start.4 = (bf16[1120,128]{1,0:T(8,128)(2,1)S(1)}, bf16[1120,128]{1,0:T(8,128)(2,1)S(1)}, u32[]{:S(2)}, u32[]{:S(2)}) collective-permute-start(bf16[1120,128]{1,0:T(8,128)(2,1)S(1)} %shard_map.69.refs_0_), channel_id=1, source_target_pairs={{2,18},{3,19},{6,22},{7,23},{10,26},{11,27},{14,30},{15,31},{16,0}... | collective-permute-start | bytes 860168 | tf_op jit(solution)/shard_map/ppermute | solution.py:416
  73.1 0.1 shard_map.73.refs_2_
  73.2 1.3 %collective-permute-start.10 = (bf16[560,128]{1,0:T(8,128)(2,1)S(1)}, bf16[560,128]{1,0:T(8,128)(2,1)S(1)}, u32[]{:S(2)}, u32[]{:S(2)}) collective-permute-start(bf16[560,128]{1,0:T(8,128)(2,1)S(1)} %shard_map.73.refs_2_), channel_id=1, source_target_pairs={{0,16},{1,17},{4,20},{5,21},{8,24},{9,25},{12,28},{13,29},{18,2},{... | collective-permute-start | bytes 430088 | tf_op jit(solution)/shard_map/ppermute | solution.py:416
  74.5 3.4 %collective-permute-done.13.refs_1_ = bf16[560,128]{1,0:T(8,128)(2,1)S(1)} collective-permute-done((bf16[560,128]{1,0:T(8,128)(2,1)S(1)}, bf16[560,128]{1,0:T(8,128)(2,1)S(1)}, u32[]{:S(2)}, u32[]{:S(2)}) %collective-permute-start.13) | collective-permute-done | bytes 143392 | tf_op jit(solution)/shard_map/ppermute | solution.py:406
  78.0 1.3 %collective-permute-start.14 = (bf16[560,128]{1,0:T(8,128)(2,1)S(1)}, bf16[560,128]{1,0:T(8,128)(2,1)S(1)}, u32[]{:S(2)}, u32[]{:S(2)}) collective-permute-start(bf16[560,128]{1,0:T(8,128)(2,1)S(1)} %shard_map.77.refs_4_), channel_id=1, source_target_pairs={{0,16},{1,17},{4,20},{5,21},{8,24},{9,25},{12,28},{13,29},{18,2},{... | collective-permute-start | bytes 430088 | tf_op jit(solution)/shard_map/ppermute | solution.py:416
  79.3 7.0 %collective-permute-done.10.refs_3_ = bf16[560,128]{1,0:T(8,128)(2,1)S(1)} collective-permute-done((bf16[560,128]{1,0:T(8,128)(2,1)S(1)}, bf16[560,128]{1,0:T(8,128)(2,1)S(1)}, u32[]{:S(2)}, u32[]{:S(2)}) %collective-permute-start.10) | collective-permute-done | bytes 143392 | tf_op jit(solution)/shard_map/ppermute | solution.py:416
  86.3 1.9 %collective-permute-done.14.refs_5_ = bf16[560,128]{1,0:T(8,128)(2,1)S(1)} collective-permute-done((bf16[560,128]{1,0:T(8,128)(2,1)S(1)}, bf16[560,128]{1,0:T(8,128)(2,1)S(1)}, u32[]{:S(2)}, u32[]{:S(2)}) %collective-permute-start.14) | collective-permute-done | bytes 143392 | tf_op jit(solution)/shard_map/ppermute | solution.py:416
  88.2 1.7 %shard_map.78 = bf16[32,32,128]{2,1,0:T(8,128)(2,1)} custom-call(bf16[1120,128]{1,0:T(8,128)(2,1)S(1)} %shard_map.69.refs_0_, bf16[1120,128]{1,0:T(8,128)(2,1)S(1)} %collective-permute-done.4.refs_1_, bf16[560,128]{1,0:T(8,128)(2,1)S(1)} %shard_map.73.refs_2_, bf16[560,128]{1,0:T(8,128)(2,1)S(1)} %collective-permute-done.10.refs_3_, ...), custom_call_target="tpu_custom_call" | custom-call | tf_op jit(solution)/shard_map/pallas_call | solution.py:341
  (21 shorter events, 0.7 us)
Async XLA Ops:
  1.6 20.3 %collective-permute-start.1 = (bf16[64,32,128]{2,1,0:T(8,128)(2,1)S(1)}, bf16[64,32,128]{2,1,0:T(8,128)(2,1)S(1)}, u32[]{:S(2)}, u32[]{:S(2)}) collective-permute-start(bf16[64,32,128]{2,1,0:T(8,128)(2,1)S(1)} %get-tuple-element.36), channel_id=1, source_target_pairs={{0,1},{1,0},{2,3},{3,2},{4,5},{5,4},{6,7},{7,6},{8,9},{9,8},{10,11... | collective-permute-start | bytes 1572872 | tf_op jit(solution)/shard_map/ppermute | solution.py:390
  1.6 34.1 %collective-permute-start.5 = (bf16[64,32,128]{2,1,0:T(8,128)(2,1)S(1)}, bf16[64,32,128]{2,1,0:T(8,128)(2,1)S(1)}, u32[]{:S(2)}, u32[]{:S(2)}) collective-permute-start(bf16[64,32,128]{2,1,0:T(8,128)(2,1)S(1)} %get-tuple-element.41), channel_id=1, source_target_pairs={{0,2},{1,3},{2,0},{3,1},{4,6},{5,7},{6,4},{7,5},{8,10},{9,11},{10,... | collective-permute-start | bytes 1572872 | tf_op jit(solution)/shard_map/ppermute | solution.py:390
  1.7 40.0 %collective-permute-start.7 = (bf16[64,32,128]{2,1,0:T(8,128)(2,1)S(1)}, bf16[64,32,128]{2,1,0:T(8,128)(2,1)S(1)}, u32[]{:S(2)}, u32[]{:S(2)}) collective-permute-start(bf16[64,32,128]{2,1,0:T(8,128)(2,1)S(1)} %get-tuple-element.44), channel_id=1, source_target_pairs={{0,3},{1,2},{2,1},{3,0},{4,7},{5,6},{6,5},{7,4},{8,11},{9,10},{10,... | collective-permute-start | bytes 1572872 | tf_op jit(solution)/shard_map/ppermute | solution.py:390
  21.7 26.0 %collective-permute-start = (bf16[1120,128]{1,0:T(8,128)(2,1)S(1)}, bf16[1120,128]{1,0:T(8,128)(2,1)S(1)}, u32[]{:S(2)}, u32[]{:S(2)}) collective-permute-start(bf16[1120,128]{1,0:T(8,128)(2,1)S(1)} %get-tuple-element.35), channel_id=1, source_target_pairs={{0,4},{4,0},{8,12},{12,8},{16,20},{20,16},{24,28},{28,24},{1,5},{5... | collective-permute-start | bytes 860168 | tf_op jit(solution)/shard_map/ppermute | solution.py:402
  35.7 12.0 %collective-permute-start.2 = (bf16[1120,128]{1,0:T(8,128)(2,1)S(1)}, bf16[1120,128]{1,0:T(8,128)(2,1)S(1)}, u32[]{:S(2)}, u32[]{:S(2)}) collective-permute-start(bf16[1120,128]{1,0:T(8,128)(2,1)S(1)} %get-tuple-element.38), channel_id=1, source_target_pairs={{0,4},{4,0},{8,12},{12,8},{16,20},{20,16},{24,28},{28,24},{1,5},{5... | collective-permute-start | bytes 860168 | tf_op jit(solution)/shard_map/ppermute | solution.py:402
  41.7 24.6 %collective-permute-start.6 = (bf16[560,128]{1,0:T(8,128)(2,1)S(1)}, bf16[560,128]{1,0:T(8,128)(2,1)S(1)}, u32[]{:S(2)}, u32[]{:S(2)}) collective-permute-start(bf16[560,128]{1,0:T(8,128)(2,1)S(1)} %get-tuple-element.43), channel_id=1, source_target_pairs={{0,4},{4,0},{8,12},{12,8},{16,20},{20,16},{24,28},{28,24},{1,5},{5... | collective-permute-start | bytes 430088 | tf_op jit(solution)/shard_map/ppermute | solution.py:402
  47.6 18.7 %collective-permute-start.8 = (bf16[560,128]{1,0:T(8,128)(2,1)S(1)}, bf16[560,128]{1,0:T(8,128)(2,1)S(1)}, u32[]{:S(2)}, u32[]{:S(2)}) collective-permute-start(bf16[560,128]{1,0:T(8,128)(2,1)S(1)} %get-tuple-element.46), channel_id=1, source_target_pairs={{0,4},{4,0},{8,12},{12,8},{16,20},{20,16},{24,28},{28,24},{1,5},{5... | collective-permute-start | bytes 430088 | tf_op jit(solution)/shard_map/ppermute | solution.py:402
  48.0 23.6 %collective-permute-start.3 = (bf16[1120,128]{1,0:T(8,128)(2,1)S(1)}, bf16[1120,128]{1,0:T(8,128)(2,1)S(1)}, u32[]{:S(2)}, u32[]{:S(2)}) collective-permute-start(bf16[1120,128]{1,0:T(8,128)(2,1)S(1)} %get-tuple-element.40), channel_id=1, source_target_pairs={{0,8},{4,12},{8,0},{12,4},{16,24},{20,28},{24,16},{28,20},{1,9},{5... | collective-permute-start | bytes 860168 | tf_op jit(solution)/shard_map/ppermute | solution.py:406
  57.1 9.4 %collective-permute-start.11 = (bf16[560,128]{1,0:T(8,128)(2,1)S(1)}, bf16[560,128]{1,0:T(8,128)(2,1)S(1)}, u32[]{:S(2)}, u32[]{:S(2)}) collective-permute-start(bf16[560,128]{1,0:T(8,128)(2,1)S(1)} %get-tuple-element.50), channel_id=1, source_target_pairs={{0,4},{4,0},{8,12},{12,8},{16,20},{20,16},{24,28},{28,24},{1,5},{5... | collective-permute-start | bytes 430088 | tf_op jit(solution)/shard_map/ppermute | solution.py:402
  66.2 5.2 %collective-permute-start.12 = (bf16[560,128]{1,0:T(8,128)(2,1)S(1)}, bf16[560,128]{1,0:T(8,128)(2,1)S(1)}, u32[]{:S(2)}, u32[]{:S(2)}) collective-permute-start(bf16[560,128]{1,0:T(8,128)(2,1)S(1)} %get-tuple-element.52), channel_id=1, source_target_pairs={{0,4},{4,0},{8,12},{12,8},{16,20},{20,16},{24,28},{28,24},{1,5},{5... | collective-permute-start | bytes 430088 | tf_op jit(solution)/shard_map/ppermute | solution.py:402
  66.5 6.6 %collective-permute-start.9 = (bf16[560,128]{1,0:T(8,128)(2,1)S(1)}, bf16[560,128]{1,0:T(8,128)(2,1)S(1)}, u32[]{:S(2)}, u32[]{:S(2)}) collective-permute-start(bf16[560,128]{1,0:T(8,128)(2,1)S(1)} %get-tuple-element.48), channel_id=1, source_target_pairs={{0,8},{4,12},{8,0},{12,4},{16,24},{20,28},{24,16},{28,20},{1,9},{5... | collective-permute-start | bytes 430088 | tf_op jit(solution)/shard_map/ppermute | solution.py:406
  71.5 6.4 %collective-permute-start.13 = (bf16[560,128]{1,0:T(8,128)(2,1)S(1)}, bf16[560,128]{1,0:T(8,128)(2,1)S(1)}, u32[]{:S(2)}, u32[]{:S(2)}) collective-permute-start(bf16[560,128]{1,0:T(8,128)(2,1)S(1)} %get-tuple-element.54), channel_id=1, source_target_pairs={{0,8},{4,12},{8,0},{12,4},{16,24},{20,28},{24,16},{28,20},{1,9},{5... | collective-permute-start | bytes 430088 | tf_op jit(solution)/shard_map/ppermute | solution.py:406
  71.8 16.4 %collective-permute-start.4 = (bf16[1120,128]{1,0:T(8,128)(2,1)S(1)}, bf16[1120,128]{1,0:T(8,128)(2,1)S(1)}, u32[]{:S(2)}, u32[]{:S(2)}) collective-permute-start(bf16[1120,128]{1,0:T(8,128)(2,1)S(1)} %shard_map.69.refs_0_), channel_id=1, source_target_pairs={{2,18},{3,19},{6,22},{7,23},{10,26},{11,27},{14,30},{15,31},{16,0}... | collective-permute-start | bytes 860168 | tf_op jit(solution)/shard_map/ppermute | solution.py:416
  73.2 13.2 %collective-permute-start.10 = (bf16[560,128]{1,0:T(8,128)(2,1)S(1)}, bf16[560,128]{1,0:T(8,128)(2,1)S(1)}, u32[]{:S(2)}, u32[]{:S(2)}) collective-permute-start(bf16[560,128]{1,0:T(8,128)(2,1)S(1)} %shard_map.73.refs_2_), channel_id=1, source_target_pairs={{0,16},{1,17},{4,20},{5,21},{8,24},{9,25},{12,28},{13,29},{18,2},{... | collective-permute-start | bytes 430088 | tf_op jit(solution)/shard_map/ppermute | solution.py:416
  78.0 10.2 %collective-permute-start.14 = (bf16[560,128]{1,0:T(8,128)(2,1)S(1)}, bf16[560,128]{1,0:T(8,128)(2,1)S(1)}, u32[]{:S(2)}, u32[]{:S(2)}) collective-permute-start(bf16[560,128]{1,0:T(8,128)(2,1)S(1)} %shard_map.77.refs_4_), channel_id=1, source_target_pairs={{0,16},{1,17},{4,20},{5,21},{8,24},{9,25},{12,28},{13,29},{18,2},{... | collective-permute-start | bytes 430088 | tf_op jit(solution)/shard_map/ppermute | solution.py:416

commit v3 on v2

--- a/solution.py
+++ b/solution.py
@@ -26,18 +26,16 @@
     return pltpu.with_memory_space_constraint(x, pltpu.HBM)
 
 
-def locate(sel_ref, g, bound):
+def locate(sel_ref, wanted):
     length = sel_ref.shape[1]
-
-    def halve(_, span):
-        low, high = span
-        mid = (low + high) // 2
-        below = jnp.logical_and(low < high, sel_ref[g, jnp.minimum(mid, length - 1)] < bound)
-        rest = jnp.logical_or(below, low >= high)
-        return jnp.where(below, mid + 1, low), jnp.where(rest, high, mid)
-
-    span = (jnp.int32(0), jnp.int32(length))
-    return lax.fori_loop(0, length.bit_length(), halve, span)[0]
+    spans = [(jnp.int32(0), jnp.int32(length)) for _ in wanted]
+    for _ in range(length.bit_length()):
+        for n, (g, bound) in enumerate(wanted):
+            low, high = spans[n]
+            mid = (low + high) >> 1
+            below = jnp.logical_and(low < high, sel_ref[g, jnp.minimum(mid, length - 1)] < bound)
+            spans[n] = jnp.where(below, mid + 1, low), jnp.where(below, high, jnp.minimum(mid, high))
+    return [low for low, _ in spans]
 
 
 def collect_kernel(block, local, sel_ref, ks_ref, vs_ref, k_hbm, v_hbm, tiles, table, scales, vbuf, ksem, vsem):
@@ -48,9 +46,10 @@
     base = lax.axis_index("ctx") * local
     spans = []
     start = jnp.int32(0)
+    bounds = locate(sel_ref, [(g, base + end) for g in range(heads) for end in (0, local)])
     for g in range(heads):
-        first = locate(sel_ref, g, base)
-        count = locate(sel_ref, g, base + local) - first
+        first = bounds[2 * g]
+        count = bounds[2 * g + 1] - first
         turns = jnp.minimum((count + PER_TILE - 1) // PER_TILE, most)
         table[g] = start
         spans.append((first, count, turns, start))
@@ -198,7 +197,7 @@
                 at = pl.ds(pl.multiple_of((x * blocks + b) * LANES, LANES), LANES)
                 total = acc[n, width : width + 1, at]
                 row = n * size + b * width
-                msgs[d][row : row + width, :] = (acc[n, :width, at] / total).astype(jnp.bfloat16)
+                msgs[d][row : row + width, :] = (acc[n, :width, at] * (1.0 / total)).astype(jnp.bfloat16)
                 lse_scr[b : b + 1, :] = m_scr[n, :, at] + jnp.log2(total)
             put_level(msgs[d], lse_scr[...], n * size + blocks * width)
 

time: 90.1 us -> 89.7 us (level)
  no operation moved by 1% of the time
where the time goes in v3:
time: 89.7 us; the launch traced here: 89.4 us
  Pallas kernels  65.6 us (73%)
  waiting for transfers between devices  17.2 us (19%)
  starting transfers between devices  6.43 us (7%)
    pallas_call x6, Pallas kernels, attend(): pl.pallas_call(functools.partial(attend_kernel, (heads, group, owners, bl...  57.5 us
    ppermute x3, waiting for transfers between devices, on_device(): got = lax.ppermute(held, ('ctx', 'head'), routes)  8.89 us
    ppermute x6, waiting for transfers between devices, on_device(): lax.ppermute(msgs[d], 'ctx', [(c, c ^ d) for c in range(ctx_size)])  4.81 us
    pallas_call x1, Pallas kernels, collect(): pl.pallas_call(functools.partial(collect_kernel, block, local), out_shape...  3.94 us
    ppermute x3, starting transfers between devices, on_device(): got = lax.ppermute(held, ('ctx', 'head'), routes)  3.89 us
    ppermute x3, waiting for transfers between devices, on_device(): got = lax.ppermute(sent, 'ctx', [(c, c ^ owners) for c in range(ctx_size)])  3.44 us
    ppermute x3, starting transfers between devices, on_device(): lax.ppermute(chunks[k], 'head', [(i, i ^ k) for i in range(head_size)])  1.91 us
  transfers between devices with their start and end apart: 15, of which 4 were waited for; matrix products, arithmetic and copies ran while one was open for 0% of the time, Pallas kernels for 70%

profile of v3, /device:TPU:4, one launch (start us, length us, event | category | flops | bytes accessed | tf_op | source)
XLA Modules:
  0.0 89.4 jit_solution(1855569164491328294)
XLA Ops:
  0.0 1.6 %shard_map.65 = (bf16[64,32,128]{2,1,0:T(8,128)(2,1)S(1)}, bf16[64,32,128]{2,1,0:T(8,128)(2,1)S(1)}, bf16[64,32,128]{2,1,0:T(8,128)(2,1)S(1)}, bf16[64,32,128]{2,1,0:T(8,128)(2,1)S(1)}) custom-call(bf16[64,128,128]{2,1,0:T(8,128)(2,1)} %q_hbm.1), custom_call_target="tpu_custom_call" | custom-call | tf_op jit(solution)/shard_map/pallas_call | solution.py:271
  1.6 0.1 collective-permute-start.5
  1.7 1.8 %collective-permute-start.7 = (bf16[64,32,128]{2,1,0:T(8,128)(2,1)S(1)}, bf16[64,32,128]{2,1,0:T(8,128)(2,1)S(1)}, u32[]{:S(2)}, u32[]{:S(2)}) collective-permute-start(bf16[64,32,128]{2,1,0:T(8,128)(2,1)S(1)} %get-tuple-element.44), channel_id=1, source_target_pairs={{0,3},{1,2},{2,1},{3,0},{4,7},{5,6},{6,5},{7,4},{8,11},{9,10},{10,... | collective-permute-start | bytes 1572872 | tf_op jit(solution)/shard_map/ppermute | solution.py:389
  3.5 3.9 %shard_map.64 = (bf16[10,1088,128]{2,1,0:T(8,128)(2,1)S(1)}, s32[3]{0:T(128)S(1)}, f32[10,8]{1,0:T(8,128)S(1)}) custom-call(s32[2,128]{1,0:T(2,128)} %sel_ref.1, f32[2,128]{1,0:T(2,128)} %ks_ref.1, f32[2,128]{1,0:T(2,128)} %vs_ref.1, bf16[2,8192,128]{2,1,0:T(8,128)(2,1)} %k_hbm.1, bf16[2,8192,128]{2,1,0:T(8,128)(2,1)} %v_hbm.1), custom_call_target="tpu_custom_call" | custom-call | bytes 6291456 | tf_op jit(solution)/shard_map/pallas_call | solution.py:108
  7.4 13.8 %shard_map.66 = (bf16[1120,128]{1,0:T(8,128)(2,1)S(1)}, bf16[1120,128]{1,0:T(8,128)(2,1)S(1)}) custom-call(s32[3]{0:T(128)S(1)} %get-tuple-element.30.table, f32[10,8]{1,0:T(8,128)S(1)} %get-tuple-element.31.scales, bf16[64,32,128]{2,1,0:T(8,128)(2,1)S(1)} %get-tuple-element.32.q_ref, bf16[10,1088,128]{2,1,0:T(8,128)(2,1)S(1)} %get-tuple-element.33.tiles), custom_call_target="tpu_custom_call" | custom-call | flops 1610612736 | bytes 4194304 | tf_op jit(solution)/shard_map/pallas_call | solution.py:359
  21.4 13.9 %shard_map.67 = (bf16[1120,128]{1,0:T(8,128)(2,1)S(1)}, bf16[1120,128]{1,0:T(8,128)(2,1)S(1)}) custom-call(s32[3]{0:T(128)S(1)} %get-tuple-element.30.table, f32[10,8]{1,0:T(8,128)S(1)} %get-tuple-element.31.scales, bf16[64,32,128]{2,1,0:T(8,128)(2,1)S(1)} %collective-permute-done.1.q_ref, bf16[10,1088,128]{2,1,0:T(8,128)(2,1)S(1)} %get-tuple-element.33.tiles), custom_call_target="tpu_custom_call" | custom-call | flops 1610612736 | bytes 4194304 | tf_op jit(solution)/shard_map/pallas_call | solution.py:359
  35.3 0.1 collective-permute-start.2
  35.3 5.9 %shard_map.70 = (bf16[560,128]{1,0:T(8,128)(2,1)S(1)}, bf16[560,128]{1,0:T(8,128)(2,1)S(1)}) custom-call(s32[3]{0:T(128)S(1)} %get-tuple-element.30.table, f32[10,8]{1,0:T(8,128)S(1)} %get-tuple-element.31.scales, bf16[64,32,128]{2,1,0:T(8,128)(2,1)S(1)} %collective-permute-done.5.q_ref, bf16[10,1088,128]{2,1,0:T(8,128)(2,1)S(1)} %get-tuple-element.33.tiles), custom_call_target="tpu_custom_call" | custom-call | flops 805306368 | bytes 4194304 | tf_op jit(solution)/shard_map/pallas_call | solution.py:359
  41.3 5.9 %shard_map.71 = (bf16[560,128]{1,0:T(8,128)(2,1)S(1)}, bf16[560,128]{1,0:T(8,128)(2,1)S(1)}) custom-call(s32[3]{0:T(128)S(1)} %get-tuple-element.30.table, f32[10,8]{1,0:T(8,128)S(1)} %get-tuple-element.31.scales, bf16[64,32,128]{2,1,0:T(8,128)(2,1)S(1)} %collective-permute-done.7.q_ref, bf16[10,1088,128]{2,1,0:T(8,128)(2,1)S(1)} %get-tuple-element.33.tiles), custom_call_target="tpu_custom_call" | custom-call | flops 805306368 | bytes 4194304 | tf_op jit(solution)/shard_map/pallas_call | solution.py:359
  47.3 0.3 shard_map.68
  47.7 9.0 %shard_map.74 = (bf16[560,128]{1,0:T(8,128)(2,1)S(1)}, bf16[560,128]{1,0:T(8,128)(2,1)S(1)}) custom-call(s32[3]{0:T(128)S(1)} %get-tuple-element.30.table, f32[10,8]{1,0:T(8,128)S(1)} %get-tuple-element.31.scales, bf16[64,32,128]{2,1,0:T(8,128)(2,1)S(1)} %collective-permute-done.5.q_ref, bf16[10,1088,128]{2,1,0:T(8,128)(2,1)S(1)} %get-tuple-element.33.tiles), custom_call_target="tpu_custom_call" | custom-call | flops 805306368 | bytes 4194304 | tf_op jit(solution)/shard_map/pallas_call | solution.py:359
  56.8 9.0 %shard_map.75 = (bf16[560,128]{1,0:T(8,128)(2,1)S(1)}, bf16[560,128]{1,0:T(8,128)(2,1)S(1)}) custom-call(s32[3]{0:T(128)S(1)} %get-tuple-element.30.table, f32[10,8]{1,0:T(8,128)S(1)} %get-tuple-element.31.scales, bf16[64,32,128]{2,1,0:T(8,128)(2,1)S(1)} %collective-permute-done.7.q_ref, bf16[10,1088,128]{2,1,0:T(8,128)(2,1)S(1)} %get-tuple-element.33.tiles), custom_call_target="tpu_custom_call" | custom-call | flops 805306368 | bytes 4194304 | tf_op jit(solution)/shard_map/pallas_call | solution.py:359
  65.9 0.2 shard_map.72
  66.1 4.8 %collective-permute-done.12.refs_3_ = bf16[560,128]{1,0:T(8,128)(2,1)S(1)} collective-permute-done((bf16[560,128]{1,0:T(8,128)(2,1)S(1)}, bf16[560,128]{1,0:T(8,128)(2,1)S(1)}, u32[]{:S(2)}, u32[]{:S(2)}) %collective-permute-start.12) | collective-permute-done | bytes 143392 | tf_op jit(solution)/shard_map/ppermute | solution.py:401
  70.9 0.1 shard_map.76
  71.2 0.1 shard_map.69.refs_0_
  71.3 1.3 %collective-permute-start.4 = (bf16[1120,128]{1,0:T(8,128)(2,1)S(1)}, bf16[1120,128]{1,0:T(8,128)(2,1)S(1)}, u32[]{:S(2)}, u32[]{:S(2)}) collective-permute-start(bf16[1120,128]{1,0:T(8,128)(2,1)S(1)} %shard_map.69.refs_0_), channel_id=1, source_target_pairs={{2,18},{3,19},{6,22},{7,23},{10,26},{11,27},{14,30},{15,31},{16,0}... | collective-permute-start | bytes 860168 | tf_op jit(solution)/shard_map/ppermute | solution.py:415
  72.7 0.1 shard_map.73.refs_2_
  72.7 1.3 %collective-permute-start.10 = (bf16[560,128]{1,0:T(8,128)(2,1)S(1)}, bf16[560,128]{1,0:T(8,128)(2,1)S(1)}, u32[]{:S(2)}, u32[]{:S(2)}) collective-permute-start(bf16[560,128]{1,0:T(8,128)(2,1)S(1)} %shard_map.73.refs_2_), channel_id=1, source_target_pairs={{0,16},{1,17},{4,20},{5,21},{8,24},{9,25},{12,28},{13,29},{18,2},{... | collective-permute-start | bytes 430088 | tf_op jit(solution)/shard_map/ppermute | solution.py:415
  74.0 3.4 %collective-permute-done.13.refs_1_ = bf16[560,128]{1,0:T(8,128)(2,1)S(1)} collective-permute-done((bf16[560,128]{1,0:T(8,128)(2,1)S(1)}, bf16[560,128]{1,0:T(8,128)(2,1)S(1)}, u32[]{:S(2)}, u32[]{:S(2)}) %collective-permute-start.13) | collective-permute-done | bytes 143392 | tf_op jit(solution)/shard_map/ppermute | solution.py:405
  77.5 1.3 %collective-permute-start.14 = (bf16[560,128]{1,0:T(8,128)(2,1)S(1)}, bf16[560,128]{1,0:T(8,128)(2,1)S(1)}, u32[]{:S(2)}, u32[]{:S(2)}) collective-permute-start(bf16[560,128]{1,0:T(8,128)(2,1)S(1)} %shard_map.77.refs_4_), channel_id=1, source_target_pairs={{0,16},{1,17},{4,20},{5,21},{8,24},{9,25},{12,28},{13,29},{18,2},{... | collective-permute-start | bytes 430088 | tf_op jit(solution)/shard_map/ppermute | solution.py:415
  78.8 7.0 %collective-permute-done.10.refs_3_ = bf16[560,128]{1,0:T(8,128)(2,1)S(1)} collective-permute-done((bf16[560,128]{1,0:T(8,128)(2,1)S(1)}, bf16[560,128]{1,0:T(8,128)(2,1)S(1)}, u32[]{:S(2)}, u32[]{:S(2)}) %collective-permute-start.10) | collective-permute-done | bytes 143392 | tf_op jit(solution)/shard_map/ppermute | solution.py:415
  85.9 1.9 %collective-permute-done.14.refs_5_ = bf16[560,128]{1,0:T(8,128)(2,1)S(1)} collective-permute-done((bf16[560,128]{1,0:T(8,128)(2,1)S(1)}, bf16[560,128]{1,0:T(8,128)(2,1)S(1)}, u32[]{:S(2)}, u32[]{:S(2)}) %collective-permute-start.14) | collective-permute-done | bytes 143392 | tf_op jit(solution)/shard_map/ppermute | solution.py:415
  87.7 1.7 %shard_map.78 = bf16[32,32,128]{2,1,0:T(8,128)(2,1)} custom-call(bf16[1120,128]{1,0:T(8,128)(2,1)S(1)} %shard_map.69.refs_0_, bf16[1120,128]{1,0:T(8,128)(2,1)S(1)} %collective-permute-done.4.refs_1_, bf16[560,128]{1,0:T(8,128)(2,1)S(1)} %shard_map.73.refs_2_, bf16[560,128]{1,0:T(8,128)(2,1)S(1)} %collective-permute-done.10.refs_3_, ...), custom_call_target="tpu_custom_call" | custom-call | tf_op jit(solution)/shard_map/pallas_call | solution.py:340
  (21 shorter events, 0.7 us)
Async XLA Ops:
  1.6 19.8 %collective-permute-start.1 = (bf16[64,32,128]{2,1,0:T(8,128)(2,1)S(1)}, bf16[64,32,128]{2,1,0:T(8,128)(2,1)S(1)}, u32[]{:S(2)}, u32[]{:S(2)}) collective-permute-start(bf16[64,32,128]{2,1,0:T(8,128)(2,1)S(1)} %get-tuple-element.36), channel_id=1, source_target_pairs={{0,1},{1,0},{2,3},{3,2},{4,5},{5,4},{6,7},{7,6},{8,9},{9,8},{10,11... | collective-permute-start | bytes 1572872 | tf_op jit(solution)/shard_map/ppermute | solution.py:389
  1.6 33.7 %collective-permute-start.5 = (bf16[64,32,128]{2,1,0:T(8,128)(2,1)S(1)}, bf16[64,32,128]{2,1,0:T(8,128)(2,1)S(1)}, u32[]{:S(2)}, u32[]{:S(2)}) collective-permute-start(bf16[64,32,128]{2,1,0:T(8,128)(2,1)S(1)} %get-tuple-element.41), channel_id=1, source_target_pairs={{0,2},{1,3},{2,0},{3,1},{4,6},{5,7},{6,4},{7,5},{8,10},{9,11},{10,... | collective-permute-start | bytes 1572872 | tf_op jit(solution)/shard_map/ppermute | solution.py:389
  1.7 39.6 %collective-permute-start.7 = (bf16[64,32,128]{2,1,0:T(8,128)(2,1)S(1)}, bf16[64,32,128]{2,1,0:T(8,128)(2,1)S(1)}, u32[]{:S(2)}, u32[]{:S(2)}) collective-permute-start(bf16[64,32,128]{2,1,0:T(8,128)(2,1)S(1)} %get-tuple-element.44), channel_id=1, source_target_pairs={{0,3},{1,2},{2,1},{3,0},{4,7},{5,6},{6,5},{7,4},{8,11},{9,10},{10,... | collective-permute-start | bytes 1572872 | tf_op jit(solution)/shard_map/ppermute | solution.py:389
  21.3 26.0 %collective-permute-start = (bf16[1120,128]{1,0:T(8,128)(2,1)S(1)}, bf16[1120,128]{1,0:T(8,128)(2,1)S(1)}, u32[]{:S(2)}, u32[]{:S(2)}) collective-permute-start(bf16[1120,128]{1,0:T(8,128)(2,1)S(1)} %get-tuple-element.35), channel_id=1, source_target_pairs={{0,4},{4,0},{8,12},{12,8},{16,20},{20,16},{24,28},{28,24},{1,5},{5... | collective-permute-start | bytes 860168 | tf_op jit(solution)/shard_map/ppermute | solution.py:401
  35.3 12.0 %collective-permute-start.2 = (bf16[1120,128]{1,0:T(8,128)(2,1)S(1)}, bf16[1120,128]{1,0:T(8,128)(2,1)S(1)}, u32[]{:S(2)}, u32[]{:S(2)}) collective-permute-start(bf16[1120,128]{1,0:T(8,128)(2,1)S(1)} %get-tuple-element.38), channel_id=1, source_target_pairs={{0,4},{4,0},{8,12},{12,8},{16,20},{20,16},{24,28},{28,24},{1,5},{5... | collective-permute-start | bytes 860168 | tf_op jit(solution)/shard_map/ppermute | solution.py:401
  41.2 24.6 %collective-permute-start.6 = (bf16[560,128]{1,0:T(8,128)(2,1)S(1)}, bf16[560,128]{1,0:T(8,128)(2,1)S(1)}, u32[]{:S(2)}, u32[]{:S(2)}) collective-permute-start(bf16[560,128]{1,0:T(8,128)(2,1)S(1)} %get-tuple-element.43), channel_id=1, source_target_pairs={{0,4},{4,0},{8,12},{12,8},{16,20},{20,16},{24,28},{28,24},{1,5},{5... | collective-permute-start | bytes 430088 | tf_op jit(solution)/shard_map/ppermute | solution.py:401
  47.2 18.7 %collective-permute-start.8 = (bf16[560,128]{1,0:T(8,128)(2,1)S(1)}, bf16[560,128]{1,0:T(8,128)(2,1)S(1)}, u32[]{:S(2)}, u32[]{:S(2)}) collective-permute-start(bf16[560,128]{1,0:T(8,128)(2,1)S(1)} %get-tuple-element.46), channel_id=1, source_target_pairs={{0,4},{4,0},{8,12},{12,8},{16,20},{20,16},{24,28},{28,24},{1,5},{5... | collective-permute-start | bytes 430088 | tf_op jit(solution)/shard_map/ppermute | solution.py:401
  47.6 23.6 %collective-permute-start.3 = (bf16[1120,128]{1,0:T(8,128)(2,1)S(1)}, bf16[1120,128]{1,0:T(8,128)(2,1)S(1)}, u32[]{:S(2)}, u32[]{:S(2)}) collective-permute-start(bf16[1120,128]{1,0:T(8,128)(2,1)S(1)} %get-tuple-element.40), channel_id=1, source_target_pairs={{0,8},{4,12},{8,0},{12,4},{16,24},{20,28},{24,16},{28,20},{1,9},{5... | collective-permute-start | bytes 860168 | tf_op jit(solution)/shard_map/ppermute | solution.py:405
  56.7 9.4 %collective-permute-start.11 = (bf16[560,128]{1,0:T(8,128)(2,1)S(1)}, bf16[560,128]{1,0:T(8,128)(2,1)S(1)}, u32[]{:S(2)}, u32[]{:S(2)}) collective-permute-start(bf16[560,128]{1,0:T(8,128)(2,1)S(1)} %get-tuple-element.50), channel_id=1, source_target_pairs={{0,4},{4,0},{8,12},{12,8},{16,20},{20,16},{24,28},{28,24},{1,5},{5... | collective-permute-start | bytes 430088 | tf_op jit(solution)/shard_map/ppermute | solution.py:401
  65.8 5.2 %collective-permute-start.12 = (bf16[560,128]{1,0:T(8,128)(2,1)S(1)}, bf16[560,128]{1,0:T(8,128)(2,1)S(1)}, u32[]{:S(2)}, u32[]{:S(2)}) collective-permute-start(bf16[560,128]{1,0:T(8,128)(2,1)S(1)} %get-tuple-element.52), channel_id=1, source_target_pairs={{0,4},{4,0},{8,12},{12,8},{16,20},{20,16},{24,28},{28,24},{1,5},{5... | collective-permute-start | bytes 430088 | tf_op jit(solution)/shard_map/ppermute | solution.py:401
  66.0 6.6 %collective-permute-start.9 = (bf16[560,128]{1,0:T(8,128)(2,1)S(1)}, bf16[560,128]{1,0:T(8,128)(2,1)S(1)}, u32[]{:S(2)}, u32[]{:S(2)}) collective-permute-start(bf16[560,128]{1,0:T(8,128)(2,1)S(1)} %get-tuple-element.48), channel_id=1, source_target_pairs={{0,8},{4,12},{8,0},{12,4},{16,24},{20,28},{24,16},{28,20},{1,9},{5... | collective-permute-start | bytes 430088 | tf_op jit(solution)/shard_map/ppermute | solution.py:405
  71.1 6.4 %collective-permute-start.13 = (bf16[560,128]{1,0:T(8,128)(2,1)S(1)}, bf16[560,128]{1,0:T(8,128)(2,1)S(1)}, u32[]{:S(2)}, u32[]{:S(2)}) collective-permute-start(bf16[560,128]{1,0:T(8,128)(2,1)S(1)} %get-tuple-element.54), channel_id=1, source_target_pairs={{0,8},{4,12},{8,0},{12,4},{16,24},{20,28},{24,16},{28,20},{1,9},{5... | collective-permute-start | bytes 430088 | tf_op jit(solution)/shard_map/ppermute | solution.py:405
  71.3 16.4 %collective-permute-start.4 = (bf16[1120,128]{1,0:T(8,128)(2,1)S(1)}, bf16[1120,128]{1,0:T(8,128)(2,1)S(1)}, u32[]{:S(2)}, u32[]{:S(2)}) collective-permute-start(bf16[1120,128]{1,0:T(8,128)(2,1)S(1)} %shard_map.69.refs_0_), channel_id=1, source_target_pairs={{2,18},{3,19},{6,22},{7,23},{10,26},{11,27},{14,30},{15,31},{16,0}... | collective-permute-start | bytes 860168 | tf_op jit(solution)/shard_map/ppermute | solution.py:415
  72.7 13.1 %collective-permute-start.10 = (bf16[560,128]{1,0:T(8,128)(2,1)S(1)}, bf16[560,128]{1,0:T(8,128)(2,1)S(1)}, u32[]{:S(2)}, u32[]{:S(2)}) collective-permute-start(bf16[560,128]{1,0:T(8,128)(2,1)S(1)} %shard_map.73.refs_2_), channel_id=1, source_target_pairs={{0,16},{1,17},{4,20},{5,21},{8,24},{9,25},{12,28},{13,29},{18,2},{... | collective-permute-start | bytes 430088 | tf_op jit(solution)/shard_map/ppermute | solution.py:415
  77.5 10.2 %collective-permute-start.14 = (bf16[560,128]{1,0:T(8,128)(2,1)S(1)}, bf16[560,128]{1,0:T(8,128)(2,1)S(1)}, u32[]{:S(2)}, u32[]{:S(2)}) collective-permute-start(bf16[560,128]{1,0:T(8,128)(2,1)S(1)} %shard_map.77.refs_4_), channel_id=1, source_target_pairs={{0,16},{1,17},{4,20},{5,21},{8,24},{9,25},{12,28},{13,29},{18,2},{... | collective-permute-start | bytes 430088 | tf_op jit(solution)/shard_map/ppermute | solution.py:415
